TPU v7x, 32 devices: a whole 2x2x4 slice. The times are simulated.
32 devices in a mesh: sub: 4 (over y, x), row: 8 (over z, core).
Axes of the slice: x: 2, y: 2, z: 4, core: 2. Of those that a mesh axis runs over, the one named last changes fastest.
Arguments:
- inverse: float32 [4, 1024, 12288], P('sub', 'row')
- sources: float32 [4, 16, 12288], P('sub', None, 'row'), may hold values from -6 to 6
- line_history: float32 [4, 32, 1024], P('sub', None, 'row'), may hold values from -6 to 6
- line_dest: int32 [4, 1024], P('sub', 'row'), may hold values from 0 to 3, as said below
- line_port: int32 [4, 1024], P('sub', 'row'), may hold values from 0 to 1023
- line_delay: int32 [4, 1024], P('sub', 'row'), may hold values from 16 to 32
- prev_voltage: float32 [4, 1024], P('sub', 'row'), may hold values from -6 to 6
- flux_start: float32 [4, 1024], P('sub', 'row'), may hold values from -3 to 3
- arrester_gain: float32 [4, 1024], P('sub', 'row'), may hold values from 0.5 to 4
- core_gain: float32 [4, 1024], P('sub', 'row'), may hold values from 0.25 to 2
- arrester_slots: int32 [4, 128], P('sub', 'row'), may hold values from 0 to 127, as said below
- core_slots: int32 [4, 128], P('sub', 'row'), may hold values from 0 to 127, as said below
Outputs:
- voltages: float32 [4, 16, 1024], P('sub', None, 'row')
- final_flux: float32 [4, 1024], P('sub', 'row')
Inputs may be any that keep to these rules, and one draw needn't show every extreme that they name: `line_dest`: a record never names its own subnetwork; among the 128 records of one device no subnetwork is named more than 86 times, and in every such block some subnetwork is named exactly 86 times. `arrester_slots`: the 16 entries of one device are distinct slots of that device's 128 ports and share no slot with that device's core entries. `core_slots`: the 16 entries of one device are distinct slots of that device's 128 ports.
All inputs are finite; a program needn't handle non-finite values.
Results may differ from a plain program's by a relative error of at most 0.0003.
Values sent between devices are 32-bit elements; how exact they have to be, the bound alone decides.
A program may use at most 64 MiB of HBM per device.

v0:
```python
import functools

import jax
import jax.numpy as jnp
from jax import lax
from jax.experimental import pallas as pl
from jax.experimental.pallas import tpu as pltpu
from jax.sharding import PartitionSpec as P

STEPS = 16
HISTORY = 32
NEWTON = 2
CHUNKS = 2
LANES = 128

half_step = 0.25
knee_volts = 1.5
cubic_term = 0.25

F32 = jnp.float32
BF16 = jnp.bfloat16
MESH = pl.DeviceIdType.MESH
NN = (((1,), (0,)), ((), ()))
NT = (((1,), (1,)), ((), ()))
HIGHEST = lax.Precision.HIGHEST


def iota(shape, axis):
    return lax.broadcasted_iota(jnp.int32, shape, axis)


def hi_lo(x):
    high = x.astype(BF16)
    return high, (x - high.astype(F32)).astype(BF16)


def stack_hi_lo(x):
    return jnp.concatenate(hi_lo(x), axis=0)


def dot(a, b, dims=NN):
    return lax.dot_general(a, b, dims, preferred_element_type=F32)


def four_terms(r):
    n, m = r.shape[0] // 2, r.shape[1] // 2
    return (r[:n, :m] + r[n:, :m]) + (r[:n, m:] + r[n:, m:])


def kernel(
    subs, rows, ports, slice_len, arrests, cores, n_small,
    inv, src, *refs,
):
    small_hbm, refs = refs[:n_small], refs[n_small:]
    out, refs = refs[0], refs[1:]
    small, refs = refs[:n_small], refs[n_small:]
    (
        m32, m2, mp32, mp2, gath, recin, rec, elem, par, fst, recout, x2, wc, fall, vo, cu, acc, hacc,
        small_sem, inv_sem, mp_sem, src_sem, line_send, line_recv, sub_send, sub_recv,
        rec_send, rec_recv, par_send, par_recv, elem_send, elem_recv, fst_send, fst_recv,
    ) = refs
    hist, dest, port, delay, prev, flux, again, cgain, aslots, cslots = small
    s = lax.axis_index("sub")
    me = lax.axis_index("row")
    z, c = me // 2, me % 2
    zn = rows // 2
    partner = z * 2 + (1 - c)
    elems = arrests + cores
    group = LANES // elems
    total = rows * elems
    halves = total // LANES
    width = slice_len // CHUNKS
    peers = subs - 1
    turns = 2 * (zn - 1)

    barrier = pltpu.get_barrier_semaphore()
    for j in range(1, rows):
        pl.semaphore_signal(barrier, inc=1, device_id=(s, lax.rem(me + j, rows)), device_id_type=MESH)
    for j in range(1, subs):
        pl.semaphore_signal(barrier, inc=1, device_id=(lax.rem(s + j, subs), me), device_id_type=MESH)

    small_copies = [
        pltpu.make_async_copy(small_hbm[i], small[i], small_sem.at[i]) for i in range(n_small)
    ]
    for copy in small_copies:
        copy.start()

    def src_copy(k):
        return pltpu.make_async_copy(
            src.at[0, :, pl.ds(k * width, width)], gath.at[k, me], src_sem.at[k]
        )

    for k in range(CHUNKS):
        src_copy(k).start()

    def mp_copy(r):
        return pltpu.make_async_copy(
            inv.at[0, :, pl.ds(r * slice_len, ports)], mp32.at[:, pl.ds(r * ports, ports)], mp_sem.at[r]
        )

    for r in range(rows):
        mp_copy(r).start()

    def inv_copy(b):
        cols = pl.ds(pl.multiple_of(b * slice_len, LANES), slice_len)
        return pltpu.make_async_copy(inv.at[0, :, cols], m32.at[:, cols], inv_sem.at[b])

    steps_z = [0]
    for j in range(1, zn):
        hop = (j + 1) // 2
        steps_z.append(hop if j % 2 == 1 else zn - hop)
    for hop in steps_z:
        zb = lax.rem(z + hop, zn)
        inv_copy(zb * 2 + c).start()
        inv_copy(zb * 2 + (1 - c)).start()

    for copy in small_copies:
        copy.wait()

    shifted = hist[0]
    shift = HISTORY - delay[...]
    bit = 1
    while bit <= HISTORY - STEPS:
        moved = pltpu.roll(shifted, HISTORY - bit, 0)
        shifted = jnp.where((shift // bit) % 2 == 1, moved, shifted)
        bit *= 2
    recout[:STEPS, :] = shifted[:STEPS, :]
    k8 = iota((8, LANES), 0)
    tags = jnp.where(k8 == 0, dest[...], jnp.where(k8 == 1, port[...] // ports, port[...] % ports))
    recout[STEPS:, :] = tags.astype(F32)

    lane16a, row16a = iota((arrests, LANES), 1), iota((arrests, LANES), 0)
    lane16c, row16c = iota((cores, LANES), 1), iota((cores, LANES), 0)
    put_a = jnp.where(lane16a % elems == row16a, 1.0, 0.0).astype(BF16)
    put_c = jnp.where(lane16c % elems == row16c + arrests, 1.0, 0.0).astype(BF16)
    slot_a = jnp.broadcast_to(aslots[...].astype(F32), (8, arrests)).astype(BF16)
    slot_c = jnp.broadcast_to(cslots[...].astype(F32), (8, cores)).astype(BF16)
    slot_row = (dot(slot_a, put_a) + dot(slot_c, put_c))[0:1, :]
    hit = iota((ports, LANES), 0).astype(F32) == slot_row
    slot_tiled = jnp.where(hit, 1.0, 0.0)
    slot_own = jnp.where(iota((ports, LANES), 1) // elems == me % group, slot_tiled, 0.0)
    r8 = iota((8, ports), 0)
    params = jnp.where(
        r8 == 0,
        iota((8, ports), 1).astype(F32),
        jnp.where(
            r8 == 1,
            again[...],
            jnp.where(r8 == 2, cgain[...], jnp.where(r8 == 3, prev[...], flux[...])),
        ),
    )
    par[me] = lax.dot_general(params, slot_own, NN, precision=HIGHEST, preferred_element_type=F32)

    for r in range(rows):
        mp_copy(r).wait()
    mp_hi, mp_lo = hi_lo(mp32[...])
    mp2[:ports, :] = mp_hi
    mp2[ports:, :] = mp_lo
    acc[...] = jnp.zeros_like(acc)
    hacc[...] = jnp.zeros_like(hacc)

    def split_block(j, carry):
        b = lax.rem(me + j, rows)
        inv_copy(b).wait()
        cols = pl.ds(pl.multiple_of(b * slice_len, LANES), slice_len)
        high, low = hi_lo(m32[:, cols])
        m2[:ports, cols] = high
        m2[ports:, cols] = low
        return carry

    def use_sources(b):
        for kind in range(CHUNKS):
            cols = pl.ds(pl.multiple_of(b * slice_len + kind * width, LANES), width)
            acc[...] += dot(stack_hi_lo(gath[kind, b]), m2[:, cols], NT)

    lax.fori_loop(0, rows, split_block, 0)
    for k in range(CHUNKS):
        src_copy(k).wait()
    use_sources(me)
    pl.semaphore_wait(barrier, rows + subs - 2)

    def remote(ref_from, ref_to, send, recv, to_sub, to_row):
        return pltpu.make_async_remote_copy(
            src_ref=ref_from, dst_ref=ref_to, send_sem=send, recv_sem=recv,
            device_id=(to_sub, to_row), device_id_type=MESH,
        )

    def sub_copy(j):
        return remote(
            recout, recin.at[peers - j], sub_send.at[j - 1], sub_recv.at[peers - j],
            lax.rem(s + j, subs), me,
        )

    def par_copy(b, at, target):
        return remote(par.at[b], par.at[b], par_send.at[at], par_recv.at[b], s, target)

    def line_copy(kind, b, way, target):
        ref = gath.at[kind, b]
        return remote(ref, ref, line_send.at[kind, b, way], line_recv.at[kind, b], s, target)

    def rec_copy(b, at, target):
        return remote(rec.at[b], rec.at[b], rec_send.at[at], rec_recv.at[b], s, target)

    def elem_copy(b, at, target):
        return remote(elem.at[b], elem.at[b], elem_send.at[at], elem_recv.at[b], s, target)

    def fst_copy(b, at, target):
        return remote(fst.at[b], fst.at[b], fst_send.at[at], fst_recv.at[b], s, target)

    for j in range(1, subs):
        sub_copy(j).start()
    for j in range(1, rows):
        par_copy(me, j - 1, lax.rem(me + j, rows)).start()
    for k in range(CHUNKS):
        @pl.when(z + 1 < zn)
        def _():
            line_copy(k, me, 0, me + 2).start()

        @pl.when(z > 0)
        def _():
            line_copy(k, me, 1, me - 2).start()

        line_copy(k, me, 2, partner).start()

    for j in range(1, subs):
        sub_copy(j).wait_recv()
    for j in range(peers):
        rec[me, j * STEPS : (j + 1) * STEPS, :] = recin[j, :STEPS, :]
    named = [
        jnp.where(
            recin[j, STEPS : STEPS + 1, :] == s.astype(F32), recin[j, STEPS + 1 : STEPS + 2, :], -1.0
        )
        for j in range(peers)
    ]
    spots = [recin[j, STEPS + 2 : STEPS + 3, :] for j in range(peers)]
    for j, row in enumerate(named + spots):
        rec[me, peers * STEPS + j : peers * STEPS + j + 1, :] = row
    for j in range(1, zn):
        rec_copy(me, zn + j - 1, lax.rem(z + j, zn) * 2 + c).start()
    rec_copy(me, z, partner).start()

    def turn(i):
        below = i % 2 == 0
        k = i // 2 + 1
        zb = jnp.where(below, z - k, z + k)
        zt = jnp.where(below, z + 1, z - 1)
        return zb, zt, jnp.logical_and(zb >= 0, zb < zn), jnp.logical_and(zt >= 0, zt < zn)

    def forward(i, carry):
        zb, zt, valid, onward = turn(i)
        b = zb * 2 + c

        @pl.when(valid)
        def _():
            for kind in range(CHUNKS):
                line_copy(kind, b, 0, partner).wait_recv()

                @pl.when(onward)
                def _():
                    line_copy(kind, b, 0, zt * 2 + c).start()

                line_copy(kind, b, 2, partner).start()

        return carry

    lax.fori_loop(0, 2, forward, 0)

    def use_records(b):
        values = jnp.concatenate([rec[b, j * STEPS : (j + 1) * STEPS, :] for j in range(peers)], axis=1)
        tag = rec[b, peers * STEPS :, :]
        owner = jnp.concatenate([tag[j : j + 1, :] for j in range(peers)], axis=1)
        spot = jnp.concatenate([tag[peers + j : peers + j + 1, :] for j in range(peers)], axis=1)
        land = jnp.where(iota((ports, peers * LANES), 0).astype(F32) == spot, 1.0, 0.0).astype(BF16)
        split = jnp.concatenate([jnp.where(owner == float(r), values, 0.0) for r in range(rows)], axis=0)
        hacc[...] += dot(stack_hi_lo(split), land, NT)

    use_records(me)
    for k in range(CHUNKS):
        line_copy(k, partner, 2, partner).wait_recv()
    use_sources(partner)

    def consume(i):
        zb, zt, valid, onward = turn(i)

        @pl.when(valid)
        def _():
            use_sources(zb * 2 + c)
            other = zb * 2 + (1 - c)
            for kind in range(CHUNKS):
                line_copy(kind, other, 2, partner).wait_recv()
            use_sources(other)

    def ring(i, carry):
        forward(i + 2, 0)
        consume(i)
        return carry

    early = min(2, turns - 2)
    lax.fori_loop(0, early, ring, 0)

    for j in range(1, rows):
        par_copy(lax.rem(me + j, rows), j - 1, partner).wait_recv()
    all_par = jnp.concatenate(
        [sum(par[h * group + i] for i in range(group)) for h in range(halves)], axis=1
    )
    slots_all = all_par[0:1, :]
    at_slot = iota((ports, total), 0).astype(F32) == slots_all
    owner_of = iota((ports, total), 1) // elems
    pick = None
    for r in range(rows):
        choose = jnp.where(jnp.logical_and(at_slot, owner_of == r), 1.0, 0.0).astype(BF16)
        term = dot(mp2[:, r * ports : (r + 1) * ports], choose)
        pick = term if pick is None else pick + term
    x2[...] = pick.astype(BF16)
    slot_cols = jnp.transpose(slot_tiled)[:elems].astype(BF16)
    elem[me] = dot(slot_cols, x2[:ports, :]) + dot(slot_cols, x2[ports:, :])
    for j in range(1, zn):
        elem_copy(me, zn + j - 1, lax.rem(z + j, zn) * 2 + c).start()
    elem_copy(me, z, partner).start()

    lax.fori_loop(early, turns - 2, ring, 0)

    def pass_on(j, carry):
        zb = lax.rem(z + j, zn)
        b = zb * 2 + c
        rec_copy(b, 0, partner).wait_recv()
        rec_copy(b, zb, partner).start()
        use_records(b)
        return carry

    lax.fori_loop(1, zn, pass_on, 0)

    def take(j, carry):
        b = lax.rem(z + j, zn) * 2 + (1 - c)
        rec_copy(b, 0, partner).wait_recv()
        use_records(b)
        return carry

    lax.fori_loop(0, zn, take, 0)

    def last(i, carry):
        consume(i)
        return carry

    lax.fori_loop(turns - 2, turns, last, 0)

    landed = hacc[: rows * STEPS, :] + hacc[rows * STEPS :, :]
    landed = jnp.concatenate([landed[r * STEPS : (r + 1) * STEPS, :] for r in range(rows)], axis=1)
    first = four_terms(acc[...] - dot(stack_hi_lo(landed), mp2[...], NT))
    mine = dot(stack_hi_lo(first), slot_own.astype(BF16))
    fst[me] = mine[:STEPS] + mine[STEPS:]
    for j in range(1, rows):
        fst_copy(me, j - 1, lax.rem(me + j, rows)).start()

    for j in range(1, zn):
        zb = lax.rem(z + j, zn)
        elem_copy(zb * 2 + c, 0, partner).wait_recv()
        elem_copy(zb * 2 + c, zb, partner).start()
    for j in range(zn):
        elem_copy(lax.rem(z + j, zn) * 2 + (1 - c), 0, partner).wait_recv()

    w = elem[...].reshape(total, total)
    self_row = jnp.sum(jnp.where(iota((total, total), 0) == iota((total, total), 1), w, 0.0), axis=0, keepdims=True)
    w_hi, w_lo = hi_lo(jnp.transpose(w))
    wc[:, :total] = w_hi
    wc[:, total:] = w_lo

    full = (8, total)
    is_arrest = iota(full, 1) % elems < arrests
    arrest_gain = jnp.where(is_arrest, jnp.broadcast_to(all_par[1:2, :], full), 0.0)
    core_gain = jnp.where(is_arrest, 0.0, jnp.broadcast_to(all_par[2:3, :], full))
    elem_self = jnp.broadcast_to(self_row, full)
    volts0 = jnp.broadcast_to(all_par[3:4, :], full)
    flux0 = jnp.broadcast_to(all_par[4:5, :], full)
    put = jnp.where(jnp.logical_and(at_slot, owner_of == me), 1.0, 0.0).astype(BF16)
    here = dot(jnp.ones((8, total), BF16), put, NT)[0:1]

    for j in range(1, subs):
        sub_copy(j).wait_send()
    for k in range(CHUNKS):
        @pl.when(z + 1 < zn)
        def _():
            line_copy(k, me, 0, partner).wait_send()

        @pl.when(z > 0)
        def _():
            line_copy(k, me, 1, partner).wait_send()

        line_copy(k, me, 2, partner).wait_send()

    def drain(i, carry):
        zb, zt, valid, onward = turn(i)
        b = zb * 2 + c

        @pl.when(valid)
        def _():
            for kind in range(CHUNKS):
                @pl.when(onward)
                def _():
                    line_copy(kind, b, 0, partner).wait_send()

                line_copy(kind, b, 2, partner).wait_send()

        return carry

    lax.fori_loop(0, turns, drain, 0)
    for j in range(1, rows):
        par_copy(me, j - 1, partner).wait_send()
    for at in range(2 * zn - 1):
        rec_copy(me, at, partner).wait_send()
        elem_copy(me, at, partner).wait_send()

    for j in range(1, rows):
        fst_copy(lax.rem(me + j, rows), j - 1, partner).wait_recv()
    fall[...] = jnp.concatenate(
        [sum(fst[h * group + i] for i in range(group)) for h in range(halves)], axis=1
    )

    def advance(t, carry):
        voltage, flux_now = carry
        first_now = jnp.broadcast_to(fall[pl.ds(t, 1), :], full)
        iterate = voltage
        for newton_pass in range(NEWTON):
            linked = flux_now + half_step * (iterate + voltage)
            ratio = iterate * (1.0 / knee_volts)
            rr = ratio * ratio
            ll = linked * linked
            current = arrest_gain * (iterate * (1.0 + rr)) + core_gain * (linked * (1.0 + cubic_term * ll))
            slope = arrest_gain * (1.0 + 3.0 * rr) + core_gain * (half_step + (half_step * 3.0 * cubic_term) * ll)
            recip = 1.0 / (1.0 + elem_self * slope)
            got = dot(stack_hi_lo(current), wc[...])
            coupled = got[:8, :total] + got[8:, :total] + got[:8, total:]
            iterate = iterate - (iterate - first_now + coupled) * recip
        vo[pl.ds(t, 1), :] = iterate[0:1]
        cu[pl.ds(t, 1), :] = current[0:1]
        return iterate, flux_now + half_step * (iterate + voltage)

    lax.fori_loop(0, STEPS, advance, (volts0, flux0), unroll=4)

    reach = four_terms(dot(stack_hi_lo(cu[...]), x2[...], NT))
    placed = dot(stack_hi_lo(vo[...]), put, NT)
    stacked = jnp.where(here > 0.5, placed[:STEPS] + placed[STEPS:], first - reach)
    out[:STEPS, :] = stacked
    summed = jnp.sum(stacked, axis=0, keepdims=True)
    last_flux = flux[...] + half_step * (prev[...] + 2.0 * summed - stacked[STEPS - 1 : STEPS])
    out[STEPS:, :] = jnp.broadcast_to(last_flux, (8, ports))
    for j in range(1, rows):
        fst_copy(me, j - 1, partner).wait_send()


def give(both, volts, last_flux):
    volts[0] = both[:STEPS, :]
    last_flux[...] = both[STEPS : STEPS + 1, :]


def on_device(subs, rows, *args):
    inverse, sources = args[0], args[1]
    ports = inverse.shape[1]
    order = inverse.shape[2]
    slice_len = sources.shape[2]
    arrests, cores = args[10].shape[1], args[11].shape[1]
    elems = arrests + cores
    total = rows * elems
    zn = rows // 2
    tag_rows = -(-2 * (subs - 1) // 8) * 8
    vmem = pl.BlockSpec(memory_space=pltpu.VMEM)
    hbm = pl.BlockSpec(memory_space=pl.ANY)
    dma = pltpu.SemaphoreType.DMA
    small = args[2:]
    both = pl.pallas_call(
        functools.partial(kernel, subs, rows, ports, slice_len, arrests, cores, len(small)),
        out_shape=jax.ShapeDtypeStruct((STEPS + 8, ports), F32),
        in_specs=[hbm] * len(args),
        out_specs=vmem,
        scratch_shapes=[pltpu.VMEM(a.shape, a.dtype) for a in small]
        + [
            pltpu.VMEM((ports, order), F32),
            pltpu.VMEM((2 * ports, order), BF16),
            pltpu.VMEM((ports, rows * ports), F32),
            pltpu.VMEM((2 * ports, rows * ports), BF16),
            pltpu.VMEM((CHUNKS, rows, STEPS, slice_len // CHUNKS), F32),
            pltpu.VMEM((subs - 1, STEPS + 8, LANES), F32),
            pltpu.VMEM((rows, (subs - 1) * STEPS + tag_rows, LANES), F32),
            pltpu.VMEM((rows, elems, total), F32),
            pltpu.VMEM((rows, 8, LANES), F32),
            pltpu.VMEM((rows, STEPS, LANES), F32),
            pltpu.VMEM((STEPS + 8, LANES), F32),
            pltpu.VMEM((2 * ports, total), BF16),
            pltpu.VMEM((total, 2 * total), BF16),
            pltpu.VMEM((STEPS, total), F32),
            pltpu.VMEM((STEPS, total), F32),
            pltpu.VMEM((STEPS, total), F32),
            pltpu.VMEM((2 * STEPS, 2 * ports), F32),
            pltpu.VMEM((2 * STEPS * rows, ports), F32),
            dma((len(small),)),
            dma((rows,)),
            dma((rows,)),
            dma((CHUNKS,)),
            dma((CHUNKS, rows, 3)),
            dma((CHUNKS, rows)),
            dma((subs - 1,)),
            dma((subs - 1,)),
            dma((2 * zn - 1,)),
            dma((rows,)),
            dma((rows - 1,)),
            dma((rows,)),
            dma((2 * zn - 1,)),
            dma((rows,)),
            dma((rows - 1,)),
            dma((rows,)),
        ],
        compiler_params=pltpu.CompilerParams(collective_id=0, has_side_effects=True),
        name="window",
    )(*args)
    return pl.pallas_call(
        give,
        out_shape=(
            jax.ShapeDtypeStruct((1, STEPS, ports), F32),
            jax.ShapeDtypeStruct((1, ports), F32),
        ),
        in_specs=[vmem],
        out_specs=(vmem, vmem),
        name="give",
    )(both)


def solution(mesh):
    subs, rows = mesh.shape["sub"], mesh.shape["row"]
    in_specs = (
        P("sub", "row", None),
        P("sub", None, "row"),
        P("sub", None, "row"),
    ) + (P("sub", "row"),) * 9
    out_specs = (P("sub", None, "row"), P("sub", "row"))
    return jax.shard_map(
        functools.partial(on_device, subs, rows),
        mesh=mesh, in_specs=in_specs, out_specs=out_specs, check_vma=False,
    )
```

profile of v0, /device:TPU:0, one launch (start us, length us, event | category | flops | bytes accessed | tf_op | source)
XLA Modules:
  0.0 36.1 jit_solution(3813548499973772210)
XLA Ops:
  0.6 34.2 %window.1.both = f32[24,128]{1,0:T(8,128)} custom-call(f32[1,128,12288]{2,1,0:T(8,128)} %inv.1, f32[1,16,1536]{2,1,0:T(8,128)} %src.1, f32[1,32,128]{2,1,0:T(8,128)} %refs_0_.1, s32[1,128]{1,0:T(1,128)} %refs_1_.1, s32[1,128]{1,0:T(1,128)} %refs_2_.1, s32[1,128]{1,0:T(1,128)} %refs_3_.1, f32[1,128]{1,0:T(1,128)} %refs_4_.1, f32[1,128]{1,0:T(1,128)} %refs_5_.1, ...), custom_call_target="tpu_custom_call" | custom-call | tf_op jit(solution)/shard_map/window/pallas_call | solution.py:470
  34.8 1.3 %give.1 = (f32[1,16,128]{2,1,0:T(8,128)}, f32[1,128]{1,0:T(1,128)}) custom-call(f32[24,128]{1,0:T(8,128)} %window.1.both), custom_call_target="tpu_custom_call" | custom-call | tf_op jit(solution)/shard_map/give/pallas_call | solution.py:515
where the time goes:
time: 36.4 us; the launch traced here: 36.1 us
  Pallas kernels  35.5 us (98%)
  between operations  0.64 us (2%)
    pallas_call x1, Pallas kernels, on_device(): pl.pallas_call(functools.partial(kernel, subs, rows, ports, slice_len, ar...  34.2 us
    pallas_call x1, Pallas kernels, on_device(): pl.pallas_call(give, out_shape=(jax.ShapeDtypeStruct((1, STEPS, ports), F...  1.31 us

commit v1 on v0

--- a/solution.py
+++ b/solution.py
@@ -12,6 +12,7 @@
 NEWTON = 2
 CHUNKS = 2
 LANES = 128
+TAGS = 3
 
 half_step = 0.25
 knee_volts = 1.5
@@ -55,9 +56,9 @@
     out, refs = refs[0], refs[1:]
     small, refs = refs[:n_small], refs[n_small:]
     (
-        m32, m2, mp32, mp2, gath, recin, rec, elem, par, fst, recout, x2, wc, fall, vo, cu, acc, hacc,
-        small_sem, inv_sem, mp_sem, src_sem, line_send, line_recv, sub_send, sub_recv,
-        rec_send, rec_recv, par_send, par_recv, elem_send, elem_recv, fst_send, fst_recv,
+        m32, m2, mp32, mp2, gath, unit, got_units, elem, fst, x2, wc, fall, vo, cu, acc, hacc,
+        small_sem, inv_sem, mp_sem, src_sem, line_send, line_recv, unit_send, unit_recv,
+        sub_send, sub_recv, both_send, both_recv, elem_send, elem_recv, fst_send, fst_recv,
     ) = refs
     hist, dest, port, delay, prev, flux, again, cgain, aslots, cslots = small
     s = lax.axis_index("sub")
@@ -105,14 +106,8 @@
         cols = pl.ds(pl.multiple_of(b * slice_len, LANES), slice_len)
         return pltpu.make_async_copy(inv.at[0, :, cols], m32.at[:, cols], inv_sem.at[b])
 
-    steps_z = [0]
-    for j in range(1, zn):
-        hop = (j + 1) // 2
-        steps_z.append(hop if j % 2 == 1 else zn - hop)
-    for hop in steps_z:
-        zb = lax.rem(z + hop, zn)
-        inv_copy(zb * 2 + c).start()
-        inv_copy(zb * 2 + (1 - c)).start()
+    for j in range(rows):
+        inv_copy(lax.rem(me + j, rows)).start()
 
     for copy in small_copies:
         copy.wait()
@@ -124,10 +119,6 @@
         moved = pltpu.roll(shifted, HISTORY - bit, 0)
         shifted = jnp.where((shift // bit) % 2 == 1, moved, shifted)
         bit *= 2
-    recout[:STEPS, :] = shifted[:STEPS, :]
-    k8 = iota((8, LANES), 0)
-    tags = jnp.where(k8 == 0, dest[...], jnp.where(k8 == 1, port[...] // ports, port[...] % ports))
-    recout[STEPS:, :] = tags.astype(F32)
 
     lane16a, row16a = iota((arrests, LANES), 1), iota((arrests, LANES), 0)
     lane16c, row16c = iota((cores, LANES), 1), iota((cores, LANES), 0)
@@ -141,15 +132,74 @@
     slot_own = jnp.where(iota((ports, LANES), 1) // elems == me % group, slot_tiled, 0.0)
     r8 = iota((8, ports), 0)
     params = jnp.where(
-        r8 == 0,
+        r8 == TAGS,
         iota((8, ports), 1).astype(F32),
         jnp.where(
-            r8 == 1,
+            r8 == TAGS + 1,
             again[...],
-            jnp.where(r8 == 2, cgain[...], jnp.where(r8 == 3, prev[...], flux[...])),
+            jnp.where(r8 == TAGS + 2, cgain[...], jnp.where(r8 == TAGS + 3, prev[...], flux[...])),
         ),
     )
-    par[me] = lax.dot_general(params, slot_own, NN, precision=HIGHEST, preferred_element_type=F32)
+    p1 = params.astype(BF16).astype(F32)
+    p2 = (params - p1).astype(BF16).astype(F32)
+    parts = dot(jnp.concatenate([p1, p2, params - p1 - p2], axis=0).astype(BF16), slot_own.astype(BF16))
+    par = (parts[:8] + parts[8:16]) + parts[16:24]
+    k8 = iota((8, LANES), 0)
+    tags = jnp.where(k8 == 0, dest[...], jnp.where(k8 == 1, port[...] // ports, port[...] % ports))
+    unit[c, z, :STEPS, :] = shifted[:STEPS, :]
+    unit[c, z, STEPS:, :] = jnp.where(k8 < TAGS, tags.astype(F32), par)
+
+    def remote(ref_from, ref_to, send, recv, to_sub, to_row):
+        return pltpu.make_async_remote_copy(
+            src_ref=ref_from, dst_ref=ref_to, send_sem=send, recv_sem=recv,
+            device_id=(to_sub, to_row), device_id_type=MESH,
+        )
+
+    def unit_copy(cc, zz, at, target):
+        ref = unit.at[cc, zz]
+        return remote(ref, ref, unit_send.at[at], unit_recv.at[cc, zz], s, target)
+
+    def line_copy(k, b, way, target):
+        ref = gath.at[k, b]
+        return remote(ref, ref, line_send.at[k, b, way], line_recv.at[k, b], s, target)
+
+    def sub_copy(j):
+        return remote(
+            unit.at[c], got_units.at[c, peers - j], sub_send.at[j - 1], sub_recv.at[peers - j],
+            lax.rem(s + j, subs), me,
+        )
+
+    def both_copy(cc):
+        return remote(got_units.at[cc], got_units.at[cc], both_send.at[0], both_recv.at[0], s, partner)
+
+    def elem_copy(b, at, target):
+        return remote(elem.at[b], elem.at[b], elem_send.at[at], elem_recv.at[b], s, target)
+
+    def fst_copy(b, at, target):
+        return remote(fst.at[b], fst.at[b], fst_send.at[at], fst_recv.at[b], s, target)
+
+    for k in range(CHUNKS):
+        src_copy(k).wait()
+    pl.semaphore_wait(barrier, rows + subs - 2)
+
+    for j in range(1, zn):
+        unit_copy(c, z, zn + j - 1, lax.rem(z + j, zn) * 2 + c).start()
+    unit_copy(c, z, z, partner).start()
+
+    def own_ways(k, act):
+        for hop in (2, 1):
+            if hop < zn:
+                @pl.when(z + hop < zn)
+                def _():
+                    act(line_copy(k, me, hop - 1, (z + hop) * 2 + c))
+
+                @pl.when(z - hop >= 0)
+                def _():
+                    act(line_copy(k, me, hop + 1, (z - hop) * 2 + c))
+        act(line_copy(k, me, 4, partner))
+
+    for k in range(CHUNKS):
+        own_ways(k, lambda copy: copy.start())
 
     for r in range(rows):
         mp_copy(r).wait()
@@ -174,136 +224,71 @@
             acc[...] += dot(stack_hi_lo(gath[kind, b]), m2[:, cols], NT)
 
     lax.fori_loop(0, rows, split_block, 0)
-    for k in range(CHUNKS):
-        src_copy(k).wait()
     use_sources(me)
-    pl.semaphore_wait(barrier, rows + subs - 2)
-
-    def remote(ref_from, ref_to, send, recv, to_sub, to_row):
-        return pltpu.make_async_remote_copy(
-            src_ref=ref_from, dst_ref=ref_to, send_sem=send, recv_sem=recv,
-            device_id=(to_sub, to_row), device_id_type=MESH,
-        )
-
-    def sub_copy(j):
-        return remote(
-            recout, recin.at[peers - j], sub_send.at[j - 1], sub_recv.at[peers - j],
-            lax.rem(s + j, subs), me,
-        )
-
-    def par_copy(b, at, target):
-        return remote(par.at[b], par.at[b], par_send.at[at], par_recv.at[b], s, target)
-
-    def line_copy(kind, b, way, target):
-        ref = gath.at[kind, b]
-        return remote(ref, ref, line_send.at[kind, b, way], line_recv.at[kind, b], s, target)
-
-    def rec_copy(b, at, target):
-        return remote(rec.at[b], rec.at[b], rec_send.at[at], rec_recv.at[b], s, target)
-
-    def elem_copy(b, at, target):
-        return remote(elem.at[b], elem.at[b], elem_send.at[at], elem_recv.at[b], s, target)
-
-    def fst_copy(b, at, target):
-        return remote(fst.at[b], fst.at[b], fst_send.at[at], fst_recv.at[b], s, target)
-
+
+    def pass_unit(j, carry):
+        zz = lax.rem(z + j, zn)
+        unit_copy(c, zz, 0, partner).wait_recv()
+        unit_copy(c, zz, zz, partner).start()
+        return carry
+
+    lax.fori_loop(1, zn, pass_unit, 0)
     for j in range(1, subs):
         sub_copy(j).start()
-    for j in range(1, rows):
-        par_copy(me, j - 1, lax.rem(me + j, rows)).start()
-    for k in range(CHUNKS):
-        @pl.when(z + 1 < zn)
-        def _():
-            line_copy(k, me, 0, me + 2).start()
-
-        @pl.when(z > 0)
-        def _():
-            line_copy(k, me, 1, me - 2).start()
-
-        line_copy(k, me, 2, partner).start()
-
-    for j in range(1, subs):
-        sub_copy(j).wait_recv()
-    for j in range(peers):
-        rec[me, j * STEPS : (j + 1) * STEPS, :] = recin[j, :STEPS, :]
-    named = [
-        jnp.where(
-            recin[j, STEPS : STEPS + 1, :] == s.astype(F32), recin[j, STEPS + 1 : STEPS + 2, :], -1.0
-        )
-        for j in range(peers)
-    ]
-    spots = [recin[j, STEPS + 2 : STEPS + 3, :] for j in range(peers)]
-    for j, row in enumerate(named + spots):
-        rec[me, peers * STEPS + j : peers * STEPS + j + 1, :] = row
-    for j in range(1, zn):
-        rec_copy(me, zn + j - 1, lax.rem(z + j, zn) * 2 + c).start()
-    rec_copy(me, z, partner).start()
 
     def turn(i):
         below = i % 2 == 0
-        k = i // 2 + 1
-        zb = jnp.where(below, z - k, z + k)
-        zt = jnp.where(below, z + 1, z - 1)
-        return zb, zt, jnp.logical_and(zb >= 0, zb < zn), jnp.logical_and(zt >= 0, zt < zn)
-
-    def forward(i, carry):
-        zb, zt, valid, onward = turn(i)
+        dist = i // 2 + 1
+        zb = jnp.where(below, z - dist, z + dist)
+        step = jnp.where(below, 1, -1)
+        return zb, dist, step, jnp.logical_and(zb >= 0, zb < zn)
+
+    def onward_ways(k, b, dist, step, act):
+        for hop in (1, 2):
+            zt = z + step * hop
+            inside = jnp.logical_and(zt >= 0, zt < zn)
+
+            @pl.when(jnp.logical_and(dist % 2 == 0, inside))
+            def _():
+                act(line_copy(k, b, hop - 1, zt * 2 + c))
+
+    def forward(i):
+        zb, dist, step, valid = turn(i)
         b = zb * 2 + c
 
         @pl.when(valid)
         def _():
-            for kind in range(CHUNKS):
-                line_copy(kind, b, 0, partner).wait_recv()
-
-                @pl.when(onward)
-                def _():
-                    line_copy(kind, b, 0, zt * 2 + c).start()
-
-                line_copy(kind, b, 2, partner).start()
-
-        return carry
-
-    lax.fori_loop(0, 2, forward, 0)
-
-    def use_records(b):
-        values = jnp.concatenate([rec[b, j * STEPS : (j + 1) * STEPS, :] for j in range(peers)], axis=1)
-        tag = rec[b, peers * STEPS :, :]
-        owner = jnp.concatenate([tag[j : j + 1, :] for j in range(peers)], axis=1)
-        spot = jnp.concatenate([tag[peers + j : peers + j + 1, :] for j in range(peers)], axis=1)
-        land = jnp.where(iota((ports, peers * LANES), 0).astype(F32) == spot, 1.0, 0.0).astype(BF16)
-        split = jnp.concatenate([jnp.where(owner == float(r), values, 0.0) for r in range(rows)], axis=0)
-        hacc[...] += dot(stack_hi_lo(split), land, NT)
-
-    use_records(me)
-    for k in range(CHUNKS):
-        line_copy(k, partner, 2, partner).wait_recv()
-    use_sources(partner)
+            for k in range(CHUNKS):
+                line_copy(k, b, 0, partner).wait_recv()
+                onward_ways(k, b, dist, step, lambda copy: copy.start())
+                line_copy(k, b, 4, partner).start()
 
     def consume(i):
-        zb, zt, valid, onward = turn(i)
+        zb, dist, step, valid = turn(i)
 
         @pl.when(valid)
         def _():
             use_sources(zb * 2 + c)
             other = zb * 2 + (1 - c)
-            for kind in range(CHUNKS):
-                line_copy(kind, other, 2, partner).wait_recv()
+            for k in range(CHUNKS):
+                line_copy(k, other, 4, partner).wait_recv()
             use_sources(other)
 
-    def ring(i, carry):
-        forward(i + 2, 0)
-        consume(i)
-        return carry
-
-    early = min(2, turns - 2)
-    lax.fori_loop(0, early, ring, 0)
-
-    for j in range(1, rows):
-        par_copy(lax.rem(me + j, rows), j - 1, partner).wait_recv()
+    for k in range(CHUNKS):
+        line_copy(k, partner, 4, partner).wait_recv()
+    use_sources(partner)
+
+    for j in range(zn):
+        zz = lax.rem(z + j, zn)
+        unit_copy(1 - c, zz, 0, partner).wait_recv()
     all_par = jnp.concatenate(
-        [sum(par[h * group + i] for i in range(group)) for h in range(halves)], axis=1
+        [
+            sum(unit[(h * group + i) % 2, (h * group + i) // 2, STEPS:, :] for i in range(group))
+            for h in range(halves)
+        ],
+        axis=1,
     )
-    slots_all = all_par[0:1, :]
+    slots_all = all_par[TAGS : TAGS + 1, :]
     at_slot = iota((ports, total), 0).astype(F32) == slots_all
     owner_of = iota((ports, total), 1) // elems
     pick = None
@@ -318,34 +303,53 @@
         elem_copy(me, zn + j - 1, lax.rem(z + j, zn) * 2 + c).start()
     elem_copy(me, z, partner).start()
 
-    lax.fori_loop(early, turns - 2, ring, 0)
-
-    def pass_on(j, carry):
-        zb = lax.rem(z + j, zn)
-        b = zb * 2 + c
-        rec_copy(b, 0, partner).wait_recv()
-        rec_copy(b, zb, partner).start()
-        use_records(b)
+    forward(0)
+    forward(1)
+
+    def ring(i, carry):
+        forward(i + 2)
+        consume(i)
         return carry
 
-    lax.fori_loop(1, zn, pass_on, 0)
-
-    def take(j, carry):
-        b = lax.rem(z + j, zn) * 2 + (1 - c)
-        rec_copy(b, 0, partner).wait_recv()
-        use_records(b)
-        return carry
-
-    lax.fori_loop(0, zn, take, 0)
+    lax.fori_loop(0, turns - 2, ring, 0)
+
+    for j in range(1, subs):
+        sub_copy(j).wait_recv()
+    both_copy(c).start()
+
+    def use_records(cc):
+        blocks = [(x, zz) for zz in range(zn) for x in range(peers)]
+        values = jnp.concatenate([got_units[cc, x, zz, :STEPS, :] for x, zz in blocks], axis=1)
+        tag = jnp.concatenate([got_units[cc, x, zz, STEPS:, :] for x, zz in blocks], axis=1)
+        owner = jnp.where(tag[0:1, :] == s.astype(F32), tag[1:2, :], -1.0)
+        spot = tag[2:3, :]
+        wide = values.shape[1]
+        land = jnp.where(iota((ports, wide), 0).astype(F32) == spot, 1.0, 0.0).astype(BF16)
+        high, low = hi_lo(values)
+        wide_owner = jnp.broadcast_to(owner, (STEPS, wide))
+        split = []
+        for r in range(rows):
+            mine = jnp.where(wide_owner == float(r), 1.0, 0.0).astype(BF16)
+            split += [high * mine, low * mine]
+        hacc[...] += dot(jnp.concatenate(split, axis=0), land, NT)
+
+    use_records(c)
 
     def last(i, carry):
         consume(i)
         return carry
 
     lax.fori_loop(turns - 2, turns, last, 0)
-
-    landed = hacc[: rows * STEPS, :] + hacc[rows * STEPS :, :]
-    landed = jnp.concatenate([landed[r * STEPS : (r + 1) * STEPS, :] for r in range(rows)], axis=1)
+    both_copy(1 - c).wait_recv()
+    use_records(1 - c)
+
+    landed = jnp.concatenate(
+        [
+            hacc[2 * r * STEPS : (2 * r + 1) * STEPS, :] + hacc[(2 * r + 1) * STEPS : (2 * r + 2) * STEPS, :]
+            for r in range(rows)
+        ],
+        axis=1,
+    )
     first = four_terms(acc[...] - dot(stack_hi_lo(landed), mp2[...], NT))
     mine = dot(stack_hi_lo(first), slot_own.astype(BF16))
     fst[me] = mine[:STEPS] + mine[STEPS:]
@@ -367,47 +371,36 @@
 
     full = (8, total)
     is_arrest = iota(full, 1) % elems < arrests
-    arrest_gain = jnp.where(is_arrest, jnp.broadcast_to(all_par[1:2, :], full), 0.0)
-    core_gain = jnp.where(is_arrest, 0.0, jnp.broadcast_to(all_par[2:3, :], full))
+    rowp = lambda i: jnp.broadcast_to(all_par[TAGS + i : TAGS + i + 1, :], full)
+    arrest_gain = jnp.where(is_arrest, rowp(1), 0.0)
+    core_gain = jnp.where(is_arrest, 0.0, rowp(2))
     elem_self = jnp.broadcast_to(self_row, full)
-    volts0 = jnp.broadcast_to(all_par[3:4, :], full)
-    flux0 = jnp.broadcast_to(all_par[4:5, :], full)
+    volts0 = rowp(3)
+    flux0 = rowp(4)
     put = jnp.where(jnp.logical_and(at_slot, owner_of == me), 1.0, 0.0).astype(BF16)
     here = dot(jnp.ones((8, total), BF16), put, NT)[0:1]
 
     for j in range(1, subs):
         sub_copy(j).wait_send()
+    both_copy(c).wait_send()
     for k in range(CHUNKS):
-        @pl.when(z + 1 < zn)
-        def _():
-            line_copy(k, me, 0, partner).wait_send()
-
-        @pl.when(z > 0)
-        def _():
-            line_copy(k, me, 1, partner).wait_send()
-
-        line_copy(k, me, 2, partner).wait_send()
+        own_ways(k, lambda copy: copy.wait_send())
 
     def drain(i, carry):
-        zb, zt, valid, onward = turn(i)
+        zb, dist, step, valid = turn(i)
         b = zb * 2 + c
 
         @pl.when(valid)
         def _():
-            for kind in range(CHUNKS):
-                @pl.when(onward)
-                def _():
-                    line_copy(kind, b, 0, partner).wait_send()
-
-                line_copy(kind, b, 2, partner).wait_send()
+            for k in range(CHUNKS):
+                onward_ways(k, b, dist, step, lambda copy: copy.wait_send())
+                line_copy(k, b, 4, partner).wait_send()
 
         return carry
 
     lax.fori_loop(0, turns, drain, 0)
-    for j in range(1, rows):
-        par_copy(me, j - 1, partner).wait_send()
     for at in range(2 * zn - 1):
-        rec_copy(me, at, partner).wait_send()
+        unit_copy(c, z, at, partner).wait_send()
         elem_copy(me, at, partner).wait_send()
 
     for j in range(1, rows):
@@ -462,7 +455,6 @@
     elems = arrests + cores
     total = rows * elems
     zn = rows // 2
-    tag_rows = -(-2 * (subs - 1) // 8) * 8
     vmem = pl.BlockSpec(memory_space=pltpu.VMEM)
     hbm = pl.BlockSpec(memory_space=pl.ANY)
     dma = pltpu.SemaphoreType.DMA
@@ -479,12 +471,10 @@
             pltpu.VMEM((ports, rows * ports), F32),
             pltpu.VMEM((2 * ports, rows * ports), BF16),
             pltpu.VMEM((CHUNKS, rows, STEPS, slice_len // CHUNKS), F32),
-            pltpu.VMEM((subs - 1, STEPS + 8, LANES), F32),
-            pltpu.VMEM((rows, (subs - 1) * STEPS + tag_rows, LANES), F32),
+            pltpu.VMEM((2, zn, STEPS + 8, LANES), F32),
+            pltpu.VMEM((2, subs - 1, zn, STEPS + 8, LANES), F32),
             pltpu.VMEM((rows, elems, total), F32),
-            pltpu.VMEM((rows, 8, LANES), F32),
             pltpu.VMEM((rows, STEPS, LANES), F32),
-            pltpu.VMEM((STEPS + 8, LANES), F32),
             pltpu.VMEM((2 * ports, total), BF16),
             pltpu.VMEM((total, 2 * total), BF16),
             pltpu.VMEM((STEPS, total), F32),
@@ -496,14 +486,14 @@
             dma((rows,)),
             dma((rows,)),
             dma((CHUNKS,)),
-            dma((CHUNKS, rows, 3)),
+            dma((CHUNKS, rows, 5)),
             dma((CHUNKS, rows)),
+            dma((2 * zn - 1,)),
+            dma((2, zn)),
             dma((subs - 1,)),
             dma((subs - 1,)),
-            dma((2 * zn - 1,)),
-            dma((rows,)),
-            dma((rows - 1,)),
-            dma((rows,)),
+            dma((1,)),
+            dma((1,)),
             dma((2 * zn - 1,)),
             dma((rows,)),
             dma((rows - 1,)),

time: 36.4 us -> 35.1 us (0.964)
  Pallas kernels: 35.5 us -> 34 us
    pallas_call x1, Pallas kernels: 34.2 us -> 32.7 us  [on_device(): pl.pallas_call(functools.partial(kernel, subs, rows, ports, slice_len, ar...]
where the time goes in v1:
time: 35.1 us; the launch traced here: 34.7 us
  Pallas kernels  34 us (97%)
  between operations  0.64 us (2%)
    pallas_call x1, Pallas kernels, on_device(): pl.pallas_call(functools.partial(kernel, subs, rows, ports, slice_len, ar...  32.7 us
    pallas_call x1, Pallas kernels, on_device(): pl.pallas_call(give, out_shape=(jax.ShapeDtypeStruct((1, STEPS, ports), F...  1.31 us

profile of v1, /device:TPU:0, one launch (start us, length us, event | category | flops | bytes accessed | tf_op | source)
XLA Modules:
  0.0 34.7 jit_solution(10942291730741423183)
XLA Ops:
  0.6 32.7 %window.1.both = f32[24,128]{1,0:T(8,128)} custom-call(f32[1,128,12288]{2,1,0:T(8,128)} %inv.1, f32[1,16,1536]{2,1,0:T(8,128)} %src.1, f32[1,32,128]{2,1,0:T(8,128)} %refs_0_.1, s32[1,128]{1,0:T(1,128)} %refs_1_.1, s32[1,128]{1,0:T(1,128)} %refs_2_.1, s32[1,128]{1,0:T(1,128)} %refs_3_.1, f32[1,128]{1,0:T(1,128)} %refs_4_.1, f32[1,128]{1,0:T(1,128)} %refs_5_.1, ...), custom_call_target="tpu_custom_call" | custom-call | tf_op jit(solution)/shard_map/window/pallas_call | solution.py:462
  33.4 1.3 %give.1 = (f32[1,16,128]{2,1,0:T(8,128)}, f32[1,128]{1,0:T(1,128)}) custom-call(f32[24,128]{1,0:T(8,128)} %window.1.both), custom_call_target="tpu_custom_call" | custom-call | tf_op jit(solution)/shard_map/give/pallas_call | solution.py:505

commit v2 on v1

--- a/solution.py
+++ b/solution.py
@@ -10,7 +10,6 @@
 STEPS = 16
 HISTORY = 32
 NEWTON = 2
-CHUNKS = 2
 LANES = 128
 TAGS = 3
 
@@ -70,7 +69,6 @@
     group = LANES // elems
     total = rows * elems
     halves = total // LANES
-    width = slice_len // CHUNKS
     peers = subs - 1
     turns = 2 * (zn - 1)
 
@@ -86,13 +84,10 @@
     for copy in small_copies:
         copy.start()
 
-    def src_copy(k):
-        return pltpu.make_async_copy(
-            src.at[0, :, pl.ds(k * width, width)], gath.at[k, me], src_sem.at[k]
-        )
-
-    for k in range(CHUNKS):
-        src_copy(k).start()
+    src_copy = pltpu.make_async_copy(src.at[0], gath.at[me], src_sem.at[0])
+    src_copy.start()
+    for copy in small_copies:
+        copy.wait()
 
     def mp_copy(r):
         return pltpu.make_async_copy(
@@ -108,9 +103,6 @@
 
     for j in range(rows):
         inv_copy(lax.rem(me + j, rows)).start()
-
-    for copy in small_copies:
-        copy.wait()
 
     shifted = hist[0]
     shift = HISTORY - delay[...]
@@ -159,9 +151,8 @@
         ref = unit.at[cc, zz]
         return remote(ref, ref, unit_send.at[at], unit_recv.at[cc, zz], s, target)
 
-    def line_copy(k, b, way, target):
-        ref = gath.at[k, b]
-        return remote(ref, ref, line_send.at[k, b, way], line_recv.at[k, b], s, target)
+    def line_copy(b, at, target):
+        return remote(gath.at[b], gath.at[b], line_send.at[at], line_recv.at[b], s, target)
 
     def sub_copy(j):
         return remote(
@@ -178,28 +169,25 @@
     def fst_copy(b, at, target):
         return remote(fst.at[b], fst.at[b], fst_send.at[at], fst_recv.at[b], s, target)
 
-    for k in range(CHUNKS):
-        src_copy(k).wait()
+    src_copy.wait()
     pl.semaphore_wait(barrier, rows + subs - 2)
 
     for j in range(1, zn):
         unit_copy(c, z, zn + j - 1, lax.rem(z + j, zn) * 2 + c).start()
     unit_copy(c, z, z, partner).start()
 
-    def own_ways(k, act):
-        for hop in (2, 1):
-            if hop < zn:
-                @pl.when(z + hop < zn)
-                def _():
-                    act(line_copy(k, me, hop - 1, (z + hop) * 2 + c))
-
-                @pl.when(z - hop >= 0)
-                def _():
-                    act(line_copy(k, me, hop + 1, (z - hop) * 2 + c))
-        act(line_copy(k, me, 4, partner))
-
-    for k in range(CHUNKS):
-        own_ways(k, lambda copy: copy.start())
+    def own_ways(act):
+        for dist in range(zn - 1, 0, -1):
+            @pl.when(z + dist < zn)
+            def _():
+                act(line_copy(me, zn + z + dist, (z + dist) * 2 + c))
+
+            @pl.when(z - dist >= 0)
+            def _():
+                act(line_copy(me, zn + z - dist, (z - dist) * 2 + c))
+
+    line_copy(me, z, partner).start()
+    own_ways(lambda copy: copy.start())
 
     for r in range(rows):
         mp_copy(r).wait()
@@ -219,9 +207,8 @@
         return carry
 
     def use_sources(b):
-        for kind in range(CHUNKS):
-            cols = pl.ds(pl.multiple_of(b * slice_len + kind * width, LANES), width)
-            acc[...] += dot(stack_hi_lo(gath[kind, b]), m2[:, cols], NT)
+        cols = pl.ds(pl.multiple_of(b * slice_len, LANES), slice_len)
+        acc[...] += dot(stack_hi_lo(gath[b]), m2[:, cols], NT)
 
     lax.fori_loop(0, rows, split_block, 0)
     use_sources(me)
@@ -236,46 +223,21 @@
     for j in range(1, subs):
         sub_copy(j).start()
 
-    def turn(i):
-        below = i % 2 == 0
-        dist = i // 2 + 1
-        zb = jnp.where(below, z - dist, z + dist)
-        step = jnp.where(below, 1, -1)
-        return zb, dist, step, jnp.logical_and(zb >= 0, zb < zn)
-
-    def onward_ways(k, b, dist, step, act):
-        for hop in (1, 2):
-            zt = z + step * hop
-            inside = jnp.logical_and(zt >= 0, zt < zn)
-
-            @pl.when(jnp.logical_and(dist % 2 == 0, inside))
+    def arrive(i, p):
+        zb = jnp.where(i % 2 == 0, z - i // 2 - 1, z + i // 2 + 1)
+        b = zb * 2 + p
+
+        @pl.when(jnp.logical_and(zb >= 0, zb < zn))
+        def _():
+            line_copy(b, zb, partner).wait_recv()
+
+            @pl.when(p == c)
             def _():
-                act(line_copy(k, b, hop - 1, zt * 2 + c))
-
-    def forward(i):
-        zb, dist, step, valid = turn(i)
-        b = zb * 2 + c
-
-        @pl.when(valid)
-        def _():
-            for k in range(CHUNKS):
-                line_copy(k, b, 0, partner).wait_recv()
-                onward_ways(k, b, dist, step, lambda copy: copy.start())
-                line_copy(k, b, 4, partner).start()
-
-    def consume(i):
-        zb, dist, step, valid = turn(i)
-
-        @pl.when(valid)
-        def _():
-            use_sources(zb * 2 + c)
-            other = zb * 2 + (1 - c)
-            for k in range(CHUNKS):
-                line_copy(k, other, 4, partner).wait_recv()
-            use_sources(other)
-
-    for k in range(CHUNKS):
-        line_copy(k, partner, 4, partner).wait_recv()
+                line_copy(b, zb, partner).start()
+
+            use_sources(b)
+
+    line_copy(partner, z, partner).wait_recv()
     use_sources(partner)
 
     for j in range(zn):
@@ -303,15 +265,11 @@
         elem_copy(me, zn + j - 1, lax.rem(z + j, zn) * 2 + c).start()
     elem_copy(me, z, partner).start()
 
-    forward(0)
-    forward(1)
-
-    def ring(i, carry):
-        forward(i + 2)
-        consume(i)
+    def near_core(q, carry):
+        arrive(turns - 1 - q, 1)
         return carry
 
-    lax.fori_loop(0, turns - 2, ring, 0)
+    lax.fori_loop(0, turns, near_core, 0)
 
     for j in range(1, subs):
         sub_copy(j).wait_recv()
@@ -335,13 +293,14 @@
 
     use_records(c)
 
-    def last(i, carry):
-        consume(i)
+    def far_core(q, carry):
+        arrive(turns - 1 - q, 0)
         return carry
 
-    lax.fori_loop(turns - 2, turns, last, 0)
+    lax.fori_loop(0, turns - 2, far_core, 0)
     both_copy(1 - c).wait_recv()
     use_records(1 - c)
+    lax.fori_loop(turns - 2, turns, far_core, 0)
 
     landed = jnp.concatenate(
         [
@@ -383,22 +342,9 @@
     for j in range(1, subs):
         sub_copy(j).wait_send()
     both_copy(c).wait_send()
-    for k in range(CHUNKS):
-        own_ways(k, lambda copy: copy.wait_send())
-
-    def drain(i, carry):
-        zb, dist, step, valid = turn(i)
-        b = zb * 2 + c
-
-        @pl.when(valid)
-        def _():
-            for k in range(CHUNKS):
-                onward_ways(k, b, dist, step, lambda copy: copy.wait_send())
-                line_copy(k, b, 4, partner).wait_send()
-
-        return carry
-
-    lax.fori_loop(0, turns, drain, 0)
+    own_ways(lambda copy: copy.wait_send())
+    for at in range(zn):
+        line_copy(me, at, partner).wait_send()
     for at in range(2 * zn - 1):
         unit_copy(c, z, at, partner).wait_send()
         elem_copy(me, at, partner).wait_send()
@@ -461,7 +407,7 @@
     small = args[2:]
     both = pl.pallas_call(
         functools.partial(kernel, subs, rows, ports, slice_len, arrests, cores, len(small)),
-        out_shape=jax.ShapeDtypeStruct((STEPS + 8, ports), F32),
+        out_shape=pltpu.VMEM((STEPS + 8, ports), F32),
         in_specs=[hbm] * len(args),
         out_specs=vmem,
         scratch_shapes=[pltpu.VMEM(a.shape, a.dtype) for a in small]
@@ -470,7 +416,7 @@
             pltpu.VMEM((2 * ports, order), BF16),
             pltpu.VMEM((ports, rows * ports), F32),
             pltpu.VMEM((2 * ports, rows * ports), BF16),
-            pltpu.VMEM((CHUNKS, rows, STEPS, slice_len // CHUNKS), F32),
+            pltpu.VMEM((rows, STEPS, slice_len), F32),
             pltpu.VMEM((2, zn, STEPS + 8, LANES), F32),
             pltpu.VMEM((2, subs - 1, zn, STEPS + 8, LANES), F32),
             pltpu.VMEM((rows, elems, total), F32),
@@ -485,9 +431,9 @@
             dma((len(small),)),
             dma((rows,)),
             dma((rows,)),
-            dma((CHUNKS,)),
-            dma((CHUNKS, rows, 5)),
-            dma((CHUNKS, rows)),
+            dma((1,)),
+            dma((2 * zn,)),
+            dma((rows,)),
             dma((2 * zn - 1,)),
             dma((2, zn)),
             dma((subs - 1,)),
@@ -511,7 +457,7 @@
         in_specs=[vmem],
         out_specs=(vmem, vmem),
         name="give",
-    )(both)
+    )(pltpu.with_memory_space_constraint(both, pltpu.VMEM))
 
 
 def solution(mesh):

time: 35.1 us -> 29.9 us (0.85)
  Pallas kernels: 34 us -> 29.1 us
    pallas_call x1, Pallas kernels: 32.7 us -> 28.5 us  [on_device(): pl.pallas_call(functools.partial(kernel, subs, rows, ports, slice_len, ar...]
    pallas_call x1, Pallas kernels: 1.31 us -> 0.6 us  [on_device(): pl.pallas_call(give, out_shape=(jax.ShapeDtypeStruct((1, STEPS, ports), F...]
where the time goes in v2:
time: 29.9 us; the launch traced here: 29.7 us
  Pallas kernels  29.1 us (97%)
  between operations  0.64 us (2%)
    pallas_call x1, Pallas kernels, on_device(): pl.pallas_call(functools.partial(kernel, subs, rows, ports, slice_len, ar...  28.5 us
    pallas_call x1, Pallas kernels, on_device(): pl.pallas_call(give, out_shape=(jax.ShapeDtypeStruct((1, STEPS, ports), F...  0.6 us

profile of v2, /device:TPU:0, one launch (start us, length us, event | category | flops | bytes accessed | tf_op | source)
XLA Modules:
  0.0 29.7 jit_solution(2481654795375879916)
XLA Ops:
  0.6 28.5 %window.1.both = f32[24,128]{1,0:T(8,128)S(1)} custom-call(f32[1,128,12288]{2,1,0:T(8,128)} %inv.1, f32[1,16,1536]{2,1,0:T(8,128)} %src.1, f32[1,32,128]{2,1,0:T(8,128)} %refs_0_.1, s32[1,128]{1,0:T(1,128)} %refs_1_.1, s32[1,128]{1,0:T(1,128)} %refs_2_.1, s32[1,128]{1,0:T(1,128)} %refs_3_.1, f32[1,128]{1,0:T(1,128)} %refs_4_.1, f32[1,128]{1,0:T(1,128)} %refs_5_.1, ...), custom_call_target="tpu_custom_call" | custom-call | tf_op jit(solution)/shard_map/window/pallas_call | solution.py:408
  29.1 0.6 %give.1 = (f32[1,16,128]{2,1,0:T(8,128)}, f32[1,128]{1,0:T(1,128)}) custom-call(f32[24,128]{1,0:T(8,128)S(1)} %window.1.both), custom_call_target="tpu_custom_call" | custom-call | tf_op jit(solution)/shard_map/give/pallas_call | solution.py:451

commit v3 on v2

--- a/solution.py
+++ b/solution.py
@@ -186,14 +186,20 @@
             def _():
                 act(line_copy(me, zn + z - dist, (z - dist) * 2 + c))
 
-    line_copy(me, z, partner).start()
-    own_ways(lambda copy: copy.start())
+    def send_sources(core):
+        @pl.when(c == core)
+        def _():
+            own_ways(lambda copy: copy.start())
+            line_copy(me, z, partner).start()
+
+    send_sources(0)
 
     for r in range(rows):
         mp_copy(r).wait()
     mp_hi, mp_lo = hi_lo(mp32[...])
     mp2[:ports, :] = mp_hi
     mp2[ports:, :] = mp_lo
+    send_sources(1)
     acc[...] = jnp.zeros_like(acc)
     hacc[...] = jnp.zeros_like(hacc)
 
@@ -223,22 +229,41 @@
     for j in range(1, subs):
         sub_copy(j).start()
 
-    def arrive(i, p):
-        zb = jnp.where(i % 2 == 0, z - i // 2 - 1, z + i // 2 + 1)
-        b = zb * 2 + p
-
-        @pl.when(jnp.logical_and(zb >= 0, zb < zn))
-        def _():
-            line_copy(b, zb, partner).wait_recv()
-
-            @pl.when(p == c)
+    zfar = jnp.where(z < zn // 2, zn - 1, 0)
+
+    def other_chips(act):
+        def body(q, carry):
+            i = turns - 1 - q
+            zb = jnp.where(i % 2 == 0, z - i // 2 - 1, z + i // 2 + 1)
+
+            @pl.when(jnp.logical_and(jnp.logical_and(zb >= 0, zb < zn), zb != zfar))
             def _():
-                line_copy(b, zb, partner).start()
-
-            use_sources(b)
+                act(zb)
+
+            return carry
+
+        lax.fori_loop(0, turns, body, 0)
+
+    def take(zb):
+        line_copy(zb * 2 + c, zb, partner).wait_recv()
+        line_copy(zb * 2 + c, zb, partner).start()
+
+    def take_passed(zb):
+        line_copy(zb * 2 + 1 - c, zb, partner).wait_recv()
 
     line_copy(partner, z, partner).wait_recv()
     use_sources(partner)
+
+    def use_own(zb):
+        use_sources(zb * 2 + c)
+
+    def use_passed(zb):
+        take_passed(zb)
+        use_sources(zb * 2 + 1 - c)
+
+    take(zfar)
+    use_own(zfar)
+    use_passed(zfar)
 
     for j in range(zn):
         zz = lax.rem(z + j, zn)
@@ -261,16 +286,6 @@
     x2[...] = pick.astype(BF16)
     slot_cols = jnp.transpose(slot_tiled)[:elems].astype(BF16)
     elem[me] = dot(slot_cols, x2[:ports, :]) + dot(slot_cols, x2[ports:, :])
-    for j in range(1, zn):
-        elem_copy(me, zn + j - 1, lax.rem(z + j, zn) * 2 + c).start()
-    elem_copy(me, z, partner).start()
-
-    def near_core(q, carry):
-        arrive(turns - 1 - q, 1)
-        return carry
-
-    lax.fori_loop(0, turns, near_core, 0)
-
     for j in range(1, subs):
         sub_copy(j).wait_recv()
     both_copy(c).start()
@@ -292,15 +307,14 @@
         hacc[...] += dot(jnp.concatenate(split, axis=0), land, NT)
 
     use_records(c)
-
-    def far_core(q, carry):
-        arrive(turns - 1 - q, 0)
-        return carry
-
-    lax.fori_loop(0, turns - 2, far_core, 0)
+    other_chips(take)
+    for j in range(1, zn):
+        elem_copy(me, zn + j - 1, lax.rem(z + j, zn) * 2 + c).start()
+    elem_copy(me, z, partner).start()
+    other_chips(use_own)
     both_copy(1 - c).wait_recv()
     use_records(1 - c)
-    lax.fori_loop(turns - 2, turns, far_core, 0)
+    other_chips(use_passed)
 
     landed = jnp.concatenate(
         [

time: 29.9 us -> 28.9 us (0.967)
  Pallas kernels: 29.1 us -> 28 us
    pallas_call x1, Pallas kernels: 28.5 us -> 27.4 us  [on_device(): pl.pallas_call(functools.partial(kernel, subs, rows, ports, slice_len, ar...]
where the time goes in v3:
time: 28.9 us; the launch traced here: 28.6 us
  Pallas kernels  28 us (97%)
  between operations  0.64 us (2%)
    pallas_call x1, Pallas kernels, on_device(): pl.pallas_call(functools.partial(kernel, subs, rows, ports, slice_len, ar...  27.4 us
    pallas_call x1, Pallas kernels, on_device(): pl.pallas_call(give, out_shape=(jax.ShapeDtypeStruct((1, STEPS, ports), F...  0.6 us

profile of v3, /device:TPU:0, one launch (start us, length us, event | category | flops | bytes accessed | tf_op | source)
XLA Modules:
  0.0 28.6 jit_solution(12917825797276804865)
XLA Ops:
  0.6 27.4 %window.1.both = f32[24,128]{1,0:T(8,128)S(1)} custom-call(f32[1,128,12288]{2,1,0:T(8,128)} %inv.1, f32[1,16,1536]{2,1,0:T(8,128)} %src.1, f32[1,32,128]{2,1,0:T(8,128)} %refs_0_.1, s32[1,128]{1,0:T(1,128)} %refs_1_.1, s32[1,128]{1,0:T(1,128)} %refs_2_.1, s32[1,128]{1,0:T(1,128)} %refs_3_.1, f32[1,128]{1,0:T(1,128)} %refs_4_.1, f32[1,128]{1,0:T(1,128)} %refs_5_.1, ...), custom_call_target="tpu_custom_call" | custom-call | tf_op jit(solution)/shard_map/window/pallas_call | solution.py:422
  28.0 0.6 %give.1 = (f32[1,16,128]{2,1,0:T(8,128)}, f32[1,128]{1,0:T(1,128)}) custom-call(f32[24,128]{1,0:T(8,128)S(1)} %window.1.both), custom_call_target="tpu_custom_call" | custom-call | tf_op jit(solution)/shard_map/give/pallas_call | solution.py:465

commit v4 on v3

v4 whole, which is shorter than its diff:
```python
import functools

import jax
import jax.numpy as jnp
from jax import lax
from jax.experimental import pallas as pl
from jax.experimental.pallas import tpu as pltpu
from jax.sharding import PartitionSpec as P

STEPS = 16
HISTORY = 32
NEWTON = 2
LANES = 128
TAGS = 3
HALVES = 2

half_step = 0.25
knee_volts = 1.5
cubic_term = 0.25

F32 = jnp.float32
BF16 = jnp.bfloat16
MESH = pl.DeviceIdType.MESH
NN = (((1,), (0,)), ((), ()))
NT = (((1,), (1,)), ((), ()))
HIGHEST = lax.Precision.HIGHEST


def iota(shape, axis):
    return lax.broadcasted_iota(jnp.int32, shape, axis)


def hi_lo(x):
    high = x.astype(BF16)
    return high, (x - high.astype(F32)).astype(BF16)


def stack_hi_lo(x):
    return jnp.concatenate(hi_lo(x), axis=0)


def dot(a, b, dims=NN):
    return lax.dot_general(a, b, dims, preferred_element_type=F32)


def four_terms(r):
    n, m = r.shape[0] // 2, r.shape[1] // 2
    return (r[:n, :m] + r[n:, :m]) + (r[:n, m:] + r[n:, m:])


def kernel(
    subs, rows, ports, slice_len, arrests, cores, n_small,
    inv, src, *refs,
):
    small_hbm, refs = refs[:n_small], refs[n_small:]
    (
        out, hist, tags_i, gains, slots, m32, m2, mp2, gath, unit, got_units, elem, fst,
        x2, wc, fall, vo, cu, acc, hacc,
        small_sem, inv_sem, line_sem, line_recv, unit_sem, sub_sem, both_sem, elem_sem, fst_sem,
    ) = refs
    s = lax.axis_index("sub")
    me = lax.axis_index("row")
    z, c = me // 2, me % 2
    zn = rows // 2
    partner = z * 2 + (1 - c)
    elems = arrests + cores
    group = LANES // elems
    total = rows * elems
    halves = total // LANES
    peers = subs - 1
    turns = 2 * (zn - 1)

    barrier = pltpu.get_barrier_semaphore()
    for j in range(1, rows):
        pl.semaphore_signal(barrier, inc=1, device_id=(s, lax.rem(me + j, rows)), device_id_type=MESH)
    for j in range(1, subs):
        pl.semaphore_signal(barrier, inc=1, device_id=(lax.rem(s + j, subs), me), device_id_type=MESH)

    ints, floats = small_hbm[1:4], small_hbm[4:8]
    pltpu.make_async_copy(small_hbm[0], hist, small_sem.at[0]).start()
    for i, ref in enumerate(ints):
        pltpu.make_async_copy(ref, tags_i.at[pl.ds(i, 1)], small_sem.at[1]).start()
    for i, ref in enumerate(floats):
        pltpu.make_async_copy(ref, gains.at[pl.ds(i, 1)], small_sem.at[2]).start()
    for i, ref in enumerate(small_hbm[8:]):
        pltpu.make_async_copy(ref, slots.at[i], small_sem.at[3]).start()
    src_copy = pltpu.make_async_copy(src.at[0], gath.at[me], small_sem.at[4])
    src_copy.start()

    def wait_all(ref, sem):
        pltpu.make_async_copy(ref, ref, sem).wait()

    wait_all(hist, small_sem.at[0])
    wait_all(tags_i.at[pl.ds(0, len(ints))], small_sem.at[1])
    wait_all(gains.at[pl.ds(0, len(floats))], small_sem.at[2])
    wait_all(slots, small_sem.at[3])
    dest, port, delay = (tags_i[i : i + 1, :] for i in range(len(ints)))
    prev, flux, again, cgain = (gains[i : i + 1, :] for i in range(len(floats)))

    span = m32.shape[1] // HALVES

    def inv_copy(h):
        cols = pl.ds(h * span, span)
        return pltpu.make_async_copy(inv.at[0, :, cols], m32.at[:, cols], inv_sem.at[h])

    for h in range(HALVES):
        inv_copy(h).start()

    shifted = hist[0]
    shift = HISTORY - delay
    bit = 1
    while bit <= HISTORY - STEPS:
        moved = pltpu.roll(shifted, HISTORY - bit, 0)
        shifted = jnp.where((shift // bit) % 2 == 1, moved, shifted)
        bit *= 2

    lane16a, row16a = iota((arrests, LANES), 1), iota((arrests, LANES), 0)
    lane16c, row16c = iota((cores, LANES), 1), iota((cores, LANES), 0)
    put_a = jnp.where(lane16a % elems == row16a, 1.0, 0.0).astype(BF16)
    put_c = jnp.where(lane16c % elems == row16c + arrests, 1.0, 0.0).astype(BF16)
    slot_a = jnp.broadcast_to(slots[0].astype(F32), (8, arrests)).astype(BF16)
    slot_c = jnp.broadcast_to(slots[1].astype(F32), (8, cores)).astype(BF16)
    slot_row = (dot(slot_a, put_a) + dot(slot_c, put_c))[0:1, :]
    hit = iota((ports, LANES), 0).astype(F32) == slot_row
    slot_tiled = jnp.where(hit, 1.0, 0.0)
    slot_own = jnp.where(iota((ports, LANES), 1) // elems == me % group, slot_tiled, 0.0)
    r8 = iota((8, ports), 0)
    params = jnp.where(
        r8 == TAGS,
        iota((8, ports), 1).astype(F32),
        jnp.where(
            r8 == TAGS + 1,
            again,
            jnp.where(r8 == TAGS + 2, cgain, jnp.where(r8 == TAGS + 3, prev, flux)),
        ),
    )
    p1 = params.astype(BF16).astype(F32)
    p2 = (params - p1).astype(BF16).astype(F32)
    parts = dot(jnp.concatenate([p1, p2, params - p1 - p2], axis=0).astype(BF16), slot_own.astype(BF16))
    par = (parts[:8] + parts[8:16]) + parts[16:24]
    k8 = iota((8, LANES), 0)
    tags = jnp.where(k8 == 0, dest, jnp.where(k8 == 1, port // ports, port % ports))
    mine_at = c * zn + z
    unit[mine_at, :STEPS, :] = shifted[:STEPS, :]
    unit[mine_at, STEPS:, :] = jnp.where(k8 < TAGS, tags.astype(F32), par)

    def remote(ref_from, ref_to, send, recv, to_sub, to_row):
        return pltpu.make_async_remote_copy(
            src_ref=ref_from, dst_ref=ref_to, send_sem=send, recv_sem=recv,
            device_id=(to_sub, to_row), device_id_type=MESH,
        )

    def unit_copy(zz, kind, target):
        ref = unit.at[c * zn + zz]
        return remote(ref, ref, unit_sem.at[0], unit_sem.at[1 + kind], s, target)

    def line_copy(b, target):
        return remote(gath.at[b], gath.at[b], line_sem.at[0], line_recv.at[b], s, target)

    def pass_copy(b):
        return remote(gath.at[b], gath.at[b], line_sem.at[1], line_recv.at[b], s, partner)

    def sub_copy(j):
        return remote(
            unit.at[pl.ds(c * zn, zn)], got_units.at[c, peers - j], sub_sem.at[0], sub_sem.at[1],
            lax.rem(s + j, subs), me,
        )

    def both_copy(cc):
        return remote(got_units.at[cc], got_units.at[cc], both_sem.at[0], both_sem.at[1], s, partner)

    def elem_copy(b, kind, target):
        return remote(elem.at[b], elem.at[b], elem_sem.at[0], elem_sem.at[1 + kind], s, target)

    def fst_copy(target):
        return remote(fst.at[me], fst.at[me], fst_sem.at[0], fst_sem.at[1], s, target)

    def sent(ref, sem):
        remote(ref, ref, sem, sem, s, partner).wait_send()

    def arrived(ref, sem):
        remote(ref, ref, sem, sem, s, partner).wait_recv()

    src_copy.wait()
    pl.semaphore_wait(barrier, rows + subs - 2)

    for j in range(1, zn):
        unit_copy(z, 0, lax.rem(z + j, zn) * 2 + c).start()
    unit_copy(z, 1, partner).start()

    for dist in [1] + list(range(zn - 1, 1, -1)):
        up, down = z + dist, z - dist

        @pl.when(jnp.logical_and(up < zn, jnp.logical_or(dist != 2, up != zn - 1)))
        def _():
            line_copy(me, up * 2 + c).start()

        @pl.when(jnp.logical_and(down >= 0, jnp.logical_or(dist != 2, down != 0)))
        def _():
            line_copy(me, down * 2 + c).start()

    pass_copy(me).start()
    lower, upper = z == 1, z == zn - 2
    relays = jnp.logical_or(lower, upper)
    skips = jnp.logical_or(z == 2, z == zn - 3)
    znear = jnp.where(z < zn // 2, z + 1, z - 1)

    acc[...] = jnp.zeros_like(acc)
    hacc[...] = jnp.zeros_like(hacc)

    def split_block(b, carry):
        cols = pl.ds(pl.multiple_of(b * slice_len, LANES), slice_len)
        high, low = hi_lo(m32[:, cols])
        m2[:ports, cols] = high
        m2[ports:, cols] = low
        at_ports = pl.ds(pl.multiple_of(b * ports, LANES), ports)
        mp2[:ports, at_ports] = high[:, :ports]
        mp2[ports:, at_ports] = low[:, :ports]
        return carry

    def use_sources(b):
        cols = pl.ds(pl.multiple_of(b * slice_len, LANES), slice_len)
        acc[...] += dot(stack_hi_lo(gath[b]), m2[:, cols], NT)

    for h in range(HALVES):
        inv_copy(h).wait()
        lax.fori_loop(h * rows // HALVES, (h + 1) * rows // HALVES, split_block, 0)
    use_sources(me)

    arrived(unit.at[pl.ds(0, zn - 1)], unit_sem.at[1])
    for j in range(1, zn):
        unit_copy(lax.rem(z + j, zn), 1, partner).start()
    for j in range(1, subs):
        sub_copy(j).start()

    def other_chips(lo, hi, act):
        def body(q, carry):
            i = jnp.where(jnp.logical_or(z == 0, z == zn - 1), turns - 1 - q, q)
            zb = jnp.where(i % 2 == 0, z - i // 2 - 1, z + i // 2 + 1)

            @pl.when(jnp.logical_and(jnp.logical_and(zb >= 0, zb < zn), zb != znear))
            def _():
                act(zb)

            return carry

        lax.fori_loop(lo, hi, body, 0)

    def take(zb):
        line_copy(zb * 2 + c, partner).wait_recv()
        pass_copy(zb * 2 + c).start()

    def use_own(zb):
        use_sources(zb * 2 + c)

    def use_passed(zb):
        pass_copy(zb * 2 + 1 - c).wait_recv()
        use_sources(zb * 2 + 1 - c)

    use_passed(z)
    line_copy(znear * 2 + c, partner).wait_recv()

    @pl.when(relays)
    def _():
        line_copy(znear * 2 + c, jnp.where(lower, z - 1, z + 1) * 2 + c).start()

    pass_copy(znear * 2 + c).start()
    use_own(znear)
    use_passed(znear)

    arrived(unit.at[pl.ds(0, zn)], unit_sem.at[2])
    all_par = jnp.concatenate(
        [
            sum(unit[(h * group + i) % 2 * zn + (h * group + i) // 2, STEPS:, :] for i in range(group))
            for h in range(halves)
        ],
        axis=1,
    )
    slots_all = all_par[TAGS : TAGS + 1, :]
    at_slot = iota((ports, total), 0).astype(F32) == slots_all
    owner_of = iota((ports, total), 1) // elems
    pick = None
    for r in range(rows):
        choose = jnp.where(jnp.logical_and(at_slot, owner_of == r), 1.0, 0.0).astype(BF16)
        term = dot(mp2[:, r * ports : (r + 1) * ports], choose)
        pick = term if pick is None else pick + term
    x2[...] = pick.astype(BF16)
    slot_cols = jnp.transpose(slot_tiled)[:elems].astype(BF16)
    elem[me] = dot(slot_cols, x2[:ports, :]) + dot(slot_cols, x2[ports:, :])
    for j in range(1, zn):
        elem_copy(me, 0, lax.rem(z + j, zn) * 2 + c).start()
    elem_copy(me, 1, partner).start()

    arrived(got_units.at[c], sub_sem.at[1])
    both_copy(c).start()

    def use_records(cc):
        blocks = [(x, zz) for zz in range(zn) for x in range(peers)]
        values = jnp.concatenate([got_units[cc, x, zz, :STEPS, :] for x, zz in blocks], axis=1)
        tag = jnp.concatenate([got_units[cc, x, zz, STEPS:, :] for x, zz in blocks], axis=1)
        owner = jnp.where(tag[0:1, :] == s.astype(F32), tag[1:2, :], -1.0)
        spot = tag[2:3, :]
        wide = values.shape[1]
        land = jnp.where(iota((ports, wide), 0).astype(F32) == spot, 1.0, 0.0).astype(BF16)
        high, low = hi_lo(values)
        wide_owner = jnp.broadcast_to(owner, (STEPS, wide))
        split = []
        for r in range(rows):
            mine = jnp.where(wide_owner == float(r), 1.0, 0.0).astype(BF16)
            split += [high * mine, low * mine]
        hacc[...] += dot(jnp.concatenate(split, axis=0), land, NT)

    use_records(c)

    def take_use(zb):
        take(zb)
        use_own(zb)

    other_chips(0, 2, take_use)
    both_copy(1 - c).wait_recv()
    use_records(1 - c)
    other_chips(2, turns, take_use)
    other_chips(0, turns, use_passed)

    landed = jnp.concatenate(
        [
            hacc[2 * r * STEPS : (2 * r + 1) * STEPS, :] + hacc[(2 * r + 1) * STEPS : (2 * r + 2) * STEPS, :]
            for r in range(rows)
        ],
        axis=1,
    )
    first = four_terms(acc[...] - dot(stack_hi_lo(landed), mp2[...], NT))
    mine = dot(stack_hi_lo(first), slot_own.astype(BF16))
    fst[me] = mine[:STEPS] + mine[STEPS:]
    for j in range(1, rows):
        fst_copy(lax.rem(me + j, rows)).start()

    arrived(elem.at[pl.ds(0, zn - 1)], elem_sem.at[1])
    for j in range(1, zn):
        elem_copy(lax.rem(z + j, zn) * 2 + c, 1, partner).start()
    arrived(elem.at[pl.ds(0, zn)], elem_sem.at[2])

    w = elem[...].reshape(total, total)
    self_row = jnp.sum(jnp.where(iota((total, total), 0) == iota((total, total), 1), w, 0.0), axis=0, keepdims=True)
    w_hi, w_lo = hi_lo(jnp.transpose(w))
    wc[:, :total] = w_hi
    wc[:, total:] = w_lo

    full = (8, total)
    is_arrest = iota(full, 1) % elems < arrests
    rowp = lambda i: jnp.broadcast_to(all_par[TAGS + i : TAGS + i + 1, :], full)
    arrest_gain = jnp.where(is_arrest, rowp(1), 0.0)
    core_gain = jnp.where(is_arrest, 0.0, rowp(2))
    elem_self = jnp.broadcast_to(self_row, full)
    volts0 = rowp(3)
    flux0 = rowp(4)
    put = jnp.where(jnp.logical_and(at_slot, owner_of == me), 1.0, 0.0).astype(BF16)
    here = dot(jnp.ones((8, total), BF16), put, NT)[0:1]

    sent(got_units.at[c], sub_sem.at[0])
    sent(got_units.at[c], both_sem.at[0])
    sent(gath.at[pl.ds(0, zn)], line_sem.at[1])
    line_sends = zn - 1 + relays.astype(jnp.int32) - skips.astype(jnp.int32)
    for n in range(zn - 2, zn + 1):
        @pl.when(line_sends == n)
        def _():
            sent(gath.at[pl.ds(0, n)], line_sem.at[0])

    sent(unit.at[pl.ds(0, 2 * zn - 1)], unit_sem.at[0])
    sent(elem.at[pl.ds(0, 2 * zn - 1)], elem_sem.at[0])
    arrived(fst.at[pl.ds(0, rows - 1)], fst_sem.at[1])
    fall[...] = jnp.concatenate(
        [sum(fst[h * group + i] for i in range(group)) for h in range(halves)], axis=1
    )

    def advance(t, carry):
        voltage, flux_now = carry
        first_now = jnp.broadcast_to(fall[pl.ds(t, 1), :], full)
        iterate = voltage
        for newton_pass in range(NEWTON):
            linked = flux_now + half_step * (iterate + voltage)
            ratio = iterate * (1.0 / knee_volts)
            rr = ratio * ratio
            ll = linked * linked
            current = arrest_gain * (iterate * (1.0 + rr)) + core_gain * (linked * (1.0 + cubic_term * ll))
            slope = arrest_gain * (1.0 + 3.0 * rr) + core_gain * (half_step + (half_step * 3.0 * cubic_term) * ll)
            recip = 1.0 / (1.0 + elem_self * slope)
            got = dot(stack_hi_lo(current), wc[...])
            coupled = got[:8, :total] + got[8:, :total] + got[:8, total:]
            iterate = iterate - (iterate - first_now + coupled) * recip
        vo[pl.ds(t, 1), :] = iterate[0:1]
        cu[pl.ds(t, 1), :] = current[0:1]
        return iterate, flux_now + half_step * (iterate + voltage)

    lax.fori_loop(0, STEPS, advance, (volts0, flux0), unroll=4)

    reach = four_terms(dot(stack_hi_lo(cu[...]), x2[...], NT))
    placed = dot(stack_hi_lo(vo[...]), put, NT)
    stacked = jnp.where(here > 0.5, placed[:STEPS] + placed[STEPS:], first - reach)
    out[:STEPS, :] = stacked
    summed = jnp.sum(stacked, axis=0, keepdims=True)
    last_flux = flux + half_step * (prev + 2.0 * summed - stacked[STEPS - 1 : STEPS])
    out[STEPS:, :] = jnp.broadcast_to(last_flux, (8, ports))
    sent(fst.at[pl.ds(0, rows - 1)], fst_sem.at[0])


def give(both, volts, last_flux):
    volts[0] = both[:STEPS, :]
    last_flux[...] = both[STEPS : STEPS + 1, :]


def on_device(subs, rows, *args):
    inverse, sources = args[0], args[1]
    ports = inverse.shape[1]
    order = inverse.shape[2]
    slice_len = sources.shape[2]
    arrests, cores = args[10].shape[1], args[11].shape[1]
    elems = arrests + cores
    total = rows * elems
    zn = rows // 2
    vmem = pl.BlockSpec(memory_space=pltpu.VMEM)
    hbm = pl.BlockSpec(memory_space=pl.ANY)
    dma = pltpu.SemaphoreType.DMA
    small = args[2:]
    both = pl.pallas_call(
        functools.partial(kernel, subs, rows, ports, slice_len, arrests, cores, len(small)),
        out_shape=pltpu.VMEM((STEPS + 8, ports), F32),
        in_specs=[hbm] * len(args),
        out_specs=vmem,
        scratch_shapes=[
            pltpu.VMEM(small[0].shape, F32),
            pltpu.VMEM((8, LANES), jnp.int32),
            pltpu.VMEM((8, LANES), F32),
            pltpu.VMEM((2, 1, arrests), jnp.int32),
            pltpu.VMEM((ports, order), F32),
            pltpu.VMEM((2 * ports, order), BF16),
            pltpu.VMEM((2 * ports, rows * ports), BF16),
            pltpu.VMEM((rows, STEPS, slice_len), F32),
            pltpu.VMEM((2 * zn, STEPS + 8, LANES), F32),
            pltpu.VMEM((2, subs - 1, zn, STEPS + 8, LANES), F32),
            pltpu.VMEM((rows, elems, total), F32),
            pltpu.VMEM((rows, STEPS, LANES), F32),
            pltpu.VMEM((2 * ports, total), BF16),
            pltpu.VMEM((total, 2 * total), BF16),
            pltpu.VMEM((STEPS, total), F32),
            pltpu.VMEM((STEPS, total), F32),
            pltpu.VMEM((STEPS, total), F32),
            pltpu.VMEM((2 * STEPS, 2 * ports), F32),
            pltpu.VMEM((2 * STEPS * rows, ports), F32),
            dma((5,)),
            dma((HALVES,)),
            dma((2,)),
            dma((rows,)),
            dma((3,)),
            dma((2,)),
            dma((2,)),
            dma((3,)),
            dma((2,)),
        ],
        compiler_params=pltpu.CompilerParams(collective_id=0, has_side_effects=True),
        name="window",
    )(*args)
    return pl.pallas_call(
        give,
        out_shape=(
            jax.ShapeDtypeStruct((1, STEPS, ports), F32),
            jax.ShapeDtypeStruct((1, ports), F32),
        ),
        in_specs=[vmem],
        out_specs=(vmem, vmem),
        name="give",
    )(pltpu.with_memory_space_constraint(both, pltpu.VMEM))


def solution(mesh):
    subs, rows = mesh.shape["sub"], mesh.shape["row"]
    in_specs = (
        P("sub", "row", None),
        P("sub", None, "row"),
        P("sub", None, "row"),
    ) + (P("sub", "row"),) * 9
    out_specs = (P("sub", None, "row"), P("sub", "row"))
    return jax.shard_map(
        functools.partial(on_device, subs, rows),
        mesh=mesh, in_specs=in_specs, out_specs=out_specs, check_vma=False,
    )
```

time: 28.9 us -> 27.1 us (0.938)
  Pallas kernels: 28 us -> 26.2 us
    pallas_call x1, Pallas kernels: 27.4 us -> 25.6 us  [on_device(): pl.pallas_call(functools.partial(kernel, subs, rows, ports, slice_len, ar...]
where the time goes in v4:
time: 27.1 us; the launch traced here: 26.9 us
  Pallas kernels  26.2 us (97%)
  between operations  0.64 us (2%)
    pallas_call x1, Pallas kernels, on_device(): pl.pallas_call(functools.partial(kernel, subs, rows, ports, slice_len, ar...  25.6 us
    pallas_call x1, Pallas kernels, on_device(): pl.pallas_call(give, out_shape=(jax.ShapeDtypeStruct((1, STEPS, ports), F...  0.6 us

profile of v4, /device:TPU:0, one launch (start us, length us, event | category | flops | bytes accessed | tf_op | source)
XLA Modules:
  0.0 26.9 jit_solution(9077675128529937739)
XLA Ops:
  0.6 25.6 %window.1.both = f32[24,128]{1,0:T(8,128)S(1)} custom-call(f32[1,128,12288]{2,1,0:T(8,128)} %inv.1, f32[1,16,1536]{2,1,0:T(8,128)} %src.1, f32[1,32,128]{2,1,0:T(8,128)} %refs_0_.1, s32[1,128]{1,0:T(1,128)} %refs_1_.1, s32[1,128]{1,0:T(1,128)} %refs_2_.1, s32[1,128]{1,0:T(1,128)} %refs_3_.1, f32[1,128]{1,0:T(1,128)} %refs_4_.1, f32[1,128]{1,0:T(1,128)} %refs_5_.1, ...), custom_call_target="tpu_custom_call" | custom-call | tf_op jit(solution)/shard_map/window/pallas_call | solution.py:425
  26.3 0.6 %give.1 = (f32[1,16,128]{2,1,0:T(8,128)}, f32[1,128]{1,0:T(1,128)}) custom-call(f32[24,128]{1,0:T(8,128)S(1)} %window.1.both), custom_call_target="tpu_custom_call" | custom-call | tf_op jit(solution)/shard_map/give/pallas_call | solution.py:463

commit v5 on v4

--- a/solution.py
+++ b/solution.py
@@ -56,7 +56,7 @@
     (
         out, hist, tags_i, gains, slots, m32, m2, mp2, gath, unit, got_units, elem, fst,
         x2, wc, fall, vo, cu, acc, hacc,
-        small_sem, inv_sem, line_sem, line_recv, unit_sem, sub_sem, both_sem, elem_sem, fst_sem,
+        small_sem, inv_sem, line_sem, line_recv, unit_sem, sub_sem, sub_in, both_sem, elem_sem, fst_sem,
     ) = refs
     s = lax.axis_index("sub")
     me = lax.axis_index("row")
@@ -73,8 +73,9 @@
     barrier = pltpu.get_barrier_semaphore()
     for j in range(1, rows):
         pl.semaphore_signal(barrier, inc=1, device_id=(s, lax.rem(me + j, rows)), device_id_type=MESH)
-    for j in range(1, subs):
-        pl.semaphore_signal(barrier, inc=1, device_id=(lax.rem(s + j, subs), me), device_id_type=MESH)
+    bits = [1 << k for k in range((subs - 1).bit_length())]
+    for bit in bits:
+        pl.semaphore_signal(barrier, inc=1, device_id=(s ^ bit, me), device_id_type=MESH)
 
     ints, floats = small_hbm[1:4], small_hbm[4:8]
     pltpu.make_async_copy(small_hbm[0], hist, small_sem.at[0]).start()
@@ -150,9 +151,9 @@
             device_id=(to_sub, to_row), device_id_type=MESH,
         )
 
-    def unit_copy(zz, kind, target):
+    def unit_copy(zz, at, target):
         ref = unit.at[c * zn + zz]
-        return remote(ref, ref, unit_sem.at[0], unit_sem.at[1 + kind], s, target)
+        return remote(ref, ref, unit_sem.at[0], unit_sem.at[1 + at], s, target)
 
     def line_copy(b, target):
         return remote(gath.at[b], gath.at[b], line_sem.at[0], line_recv.at[b], s, target)
@@ -160,11 +161,11 @@
     def pass_copy(b):
         return remote(gath.at[b], gath.at[b], line_sem.at[1], line_recv.at[b], s, partner)
 
-    def sub_copy(j):
-        return remote(
-            unit.at[pl.ds(c * zn, zn)], got_units.at[c, peers - j], sub_sem.at[0], sub_sem.at[1],
-            lax.rem(s + j, subs), me,
-        )
+    def send_subs(zz):
+        for j in range(1, subs):
+            remote(
+                unit.at[c * zn + zz], got_units.at[c, j - 1, zz], sub_sem.at[0], sub_sem.at[1], s ^ j, me
+            ).start()
 
     def both_copy(cc):
         return remote(got_units.at[cc], got_units.at[cc], both_sem.at[0], both_sem.at[1], s, partner)
@@ -182,11 +183,17 @@
         remote(ref, ref, sem, sem, s, partner).wait_recv()
 
     src_copy.wait()
-    pl.semaphore_wait(barrier, rows + subs - 2)
+    pl.semaphore_wait(barrier, rows - 1 + len(bits))
+
+    def tell_subs(k):
+        for bit in bits:
+            pl.semaphore_signal(sub_in.at[k], inc=1, device_id=(s ^ bit, me), device_id_type=MESH)
+
+    tell_subs(0)
 
     for j in range(1, zn):
-        unit_copy(z, 0, lax.rem(z + j, zn) * 2 + c).start()
-    unit_copy(z, 1, partner).start()
+        unit_copy(z, z, lax.rem(z + j, zn) * 2 + c).start()
+    unit_copy(z, zn, partner).start()
 
     for dist in [1] + list(range(zn - 1, 1, -1)):
         up, down = z + dist, z - dist
@@ -227,11 +234,17 @@
         lax.fori_loop(h * rows // HALVES, (h + 1) * rows // HALVES, split_block, 0)
     use_sources(me)
 
-    arrived(unit.at[pl.ds(0, zn - 1)], unit_sem.at[1])
+    for k in range(len(bits) - 1):
+        pl.semaphore_wait(sub_in.at[k], len(bits))
+        if k < len(bits) - 2:
+            tell_subs(k + 1)
+    send_subs(z)
+    toward = jnp.where(z < zn // 2, 1, zn - 1)
     for j in range(1, zn):
-        unit_copy(lax.rem(z + j, zn), 1, partner).start()
-    for j in range(1, subs):
-        sub_copy(j).start()
+        zz = lax.rem(z + j * toward, zn)
+        unit_copy(zz, zz, partner).wait_recv()
+        unit_copy(zz, zn, partner).start()
+        send_subs(zz)
 
     def other_chips(lo, hi, act):
         def body(q, carry):
@@ -268,7 +281,7 @@
     use_own(znear)
     use_passed(znear)
 
-    arrived(unit.at[pl.ds(0, zn)], unit_sem.at[2])
+    arrived(unit.at[pl.ds(0, zn)], unit_sem.at[1 + zn])
     all_par = jnp.concatenate(
         [
             sum(unit[(h * group + i) % 2 * zn + (h * group + i) // 2, STEPS:, :] for i in range(group))
@@ -451,8 +464,9 @@
             dma((HALVES,)),
             dma((2,)),
             dma((rows,)),
-            dma((3,)),
+            dma((zn + 2,)),
             dma((2,)),
+            pltpu.SemaphoreType.REGULAR((max((subs - 1).bit_length() - 1, 1),)),
             dma((2,)),
             dma((3,)),
             dma((2,)),

time: 27.1 us -> 27 us (level)
  no operation moved by 1% of the time
where the time goes in v5:
time: 27 us; the launch traced here: 26.8 us
  Pallas kernels  26.1 us (97%)
  between operations  0.64 us (2%)
    pallas_call x1, Pallas kernels, on_device(): pl.pallas_call(functools.partial(kernel, subs, rows, ports, slice_len, ar...  25.5 us
    pallas_call x1, Pallas kernels, on_device(): pl.pallas_call(give, out_shape=(jax.ShapeDtypeStruct((1, STEPS, ports), F...  0.6 us

profile of v5, /device:TPU:0, one launch (start us, length us, event | category | flops | bytes accessed | tf_op | source)
XLA Modules:
  0.0 26.8 jit_solution(3645195079180431456)
XLA Ops:
  0.6 25.5 %window.1.both = f32[24,128]{1,0:T(8,128)S(1)} custom-call(f32[1,128,12288]{2,1,0:T(8,128)} %inv.1, f32[1,16,1536]{2,1,0:T(8,128)} %src.1, f32[1,32,128]{2,1,0:T(8,128)} %refs_0_.1, s32[1,128]{1,0:T(1,128)} %refs_1_.1, s32[1,128]{1,0:T(1,128)} %refs_2_.1, s32[1,128]{1,0:T(1,128)} %refs_3_.1, f32[1,128]{1,0:T(1,128)} %refs_4_.1, f32[1,128]{1,0:T(1,128)} %refs_5_.1, ...), custom_call_target="tpu_custom_call" | custom-call | tf_op jit(solution)/shard_map/window/pallas_call | solution.py:438
  26.1 0.6 %give.1 = (f32[1,16,128]{2,1,0:T(8,128)}, f32[1,128]{1,0:T(1,128)}) custom-call(f32[24,128]{1,0:T(8,128)S(1)} %window.1.both), custom_call_target="tpu_custom_call" | custom-call | tf_op jit(solution)/shard_map/give/pallas_call | solution.py:477

commit v6 on v5

--- a/solution.py
+++ b/solution.py
@@ -13,6 +13,7 @@
 LANES = 128
 TAGS = 3
 HALVES = 2
+PART = STEPS // 2
 
 half_step = 0.25
 knee_volts = 1.5
@@ -158,6 +159,14 @@
     def line_copy(b, target):
         return remote(gath.at[b], gath.at[b], line_sem.at[0], line_recv.at[b], s, target)
 
+    def part_copy(h, b, target):
+        ref = gath.at[b, pl.ds(h * PART, PART)]
+        return remote(ref, ref, line_sem.at[0], line_recv.at[b if h == 0 else rows], s, target)
+
+    def relay_copy(h, b, target):
+        ref = gath.at[b, pl.ds(h * PART, PART)]
+        return remote(ref, ref, line_sem.at[0], line_recv.at[b], s, target)
+
     def pass_copy(b):
         return remote(gath.at[b], gath.at[b], line_sem.at[1], line_recv.at[b], s, partner)
 
@@ -195,16 +204,32 @@
         unit_copy(z, z, lax.rem(z + j, zn) * 2 + c).start()
     unit_copy(z, zn, partner).start()
 
+    def send_near(target, relayed):
+        @pl.when(relayed)
+        def _():
+            for h in range(2):
+                part_copy(h, me, target).start()
+
+        @pl.when(jnp.logical_not(relayed))
+        def _():
+            line_copy(me, target).start()
+
     for dist in [1] + list(range(zn - 1, 1, -1)):
         up, down = z + dist, z - dist
 
         @pl.when(jnp.logical_and(up < zn, jnp.logical_or(dist != 2, up != zn - 1)))
         def _():
-            line_copy(me, up * 2 + c).start()
+            if dist == 1:
+                send_near(up * 2 + c, up == zn - 2)
+            else:
+                line_copy(me, up * 2 + c).start()
 
         @pl.when(jnp.logical_and(down >= 0, jnp.logical_or(dist != 2, down != 0)))
         def _():
-            line_copy(me, down * 2 + c).start()
+            if dist == 1:
+                send_near(down * 2 + c, down == 1)
+            else:
+                line_copy(me, down * 2 + c).start()
 
     pass_copy(me).start()
     lower, upper = z == 1, z == zn - 2
@@ -212,7 +237,6 @@
     skips = jnp.logical_or(z == 2, z == zn - 3)
     znear = jnp.where(z < zn // 2, z + 1, z - 1)
 
-    acc[...] = jnp.zeros_like(acc)
     hacc[...] = jnp.zeros_like(hacc)
 
     def split_block(b, carry):
@@ -225,14 +249,18 @@
         mp2[ports:, at_ports] = low[:, :ports]
         return carry
 
+    def columns(b, count):
+        return pl.ds(pl.multiple_of(b * slice_len, LANES), count * slice_len)
+
     def use_sources(b):
-        cols = pl.ds(pl.multiple_of(b * slice_len, LANES), slice_len)
-        acc[...] += dot(stack_hi_lo(gath[b]), m2[:, cols], NT)
+        acc[...] += dot(stack_hi_lo(gath[b]), m2[:, columns(b, 1)], NT)
 
     for h in range(HALVES):
         inv_copy(h).wait()
         lax.fori_loop(h * rows // HALVES, (h + 1) * rows // HALVES, split_block, 0)
-    use_sources(me)
+    pass_copy(partner).wait_recv()
+    home = jnp.concatenate([gath[z * 2], gath[z * 2 + 1]], axis=1)
+    acc[...] = dot(stack_hi_lo(home), m2[:, columns(z * 2, 2)], NT)
 
     for k in range(len(bits) - 1):
         pl.semaphore_wait(sub_in.at[k], len(bits))
@@ -270,12 +298,18 @@
         pass_copy(zb * 2 + 1 - c).wait_recv()
         use_sources(zb * 2 + 1 - c)
 
-    use_passed(z)
-    line_copy(znear * 2 + c, partner).wait_recv()
+    near = znear * 2 + c
+    outer = jnp.where(lower, z - 1, z + 1) * 2 + c
 
     @pl.when(relays)
     def _():
-        line_copy(znear * 2 + c, jnp.where(lower, z - 1, z + 1) * 2 + c).start()
+        for h in range(2):
+            part_copy(h, near, partner).wait_recv()
+            relay_copy(h, near, outer).start()
+
+    @pl.when(jnp.logical_not(relays))
+    def _():
+        line_copy(near, partner).wait_recv()
 
     pass_copy(znear * 2 + c).start()
     use_own(znear)
@@ -292,18 +326,21 @@
     slots_all = all_par[TAGS : TAGS + 1, :]
     at_slot = iota((ports, total), 0).astype(F32) == slots_all
     owner_of = iota((ports, total), 1) // elems
-    pick = None
-    for r in range(rows):
-        choose = jnp.where(jnp.logical_and(at_slot, owner_of == r), 1.0, 0.0).astype(BF16)
-        term = dot(mp2[:, r * ports : (r + 1) * ports], choose)
-        pick = term if pick is None else pick + term
-    x2[...] = pick.astype(BF16)
+    choose = [
+        jnp.where(jnp.logical_and(at_slot, owner_of == r), 1.0, 0.0).astype(BF16) for r in range(rows)
+    ]
+    x2[...] = dot(mp2[...], jnp.concatenate(choose, axis=0)).astype(BF16)
     slot_cols = jnp.transpose(slot_tiled)[:elems].astype(BF16)
     elem[me] = dot(slot_cols, x2[:ports, :]) + dot(slot_cols, x2[ports:, :])
     for j in range(1, zn):
         elem_copy(me, 0, lax.rem(z + j, zn) * 2 + c).start()
     elem_copy(me, 1, partner).start()
 
+    def take_use(zb):
+        take(zb)
+        use_own(zb)
+
+    other_chips(0, 2, take_use)
     arrived(got_units.at[c], sub_sem.at[1])
     both_copy(c).start()
 
@@ -324,16 +361,11 @@
         hacc[...] += dot(jnp.concatenate(split, axis=0), land, NT)
 
     use_records(c)
-
-    def take_use(zb):
-        take(zb)
-        use_own(zb)
-
-    other_chips(0, 2, take_use)
+    other_chips(2, turns, take_use)
+    other_chips(0, 2, use_passed)
     both_copy(1 - c).wait_recv()
     use_records(1 - c)
-    other_chips(2, turns, take_use)
-    other_chips(0, turns, use_passed)
+    other_chips(2, turns, use_passed)
 
     landed = jnp.concatenate(
         [
@@ -399,13 +431,14 @@
             slope = arrest_gain * (1.0 + 3.0 * rr) + core_gain * (half_step + (half_step * 3.0 * cubic_term) * ll)
             recip = 1.0 / (1.0 + elem_self * slope)
             got = dot(stack_hi_lo(current), wc[...])
-            coupled = got[:8, :total] + got[8:, :total] + got[:8, total:]
-            iterate = iterate - (iterate - first_now + coupled) * recip
+            settled = iterate - (iterate - first_now) * recip
+            coupled = (got[:8, :total] + got[8:, :total]) + got[:8, total:]
+            iterate = settled - coupled * recip
         vo[pl.ds(t, 1), :] = iterate[0:1]
         cu[pl.ds(t, 1), :] = current[0:1]
         return iterate, flux_now + half_step * (iterate + voltage)
 
-    lax.fori_loop(0, STEPS, advance, (volts0, flux0), unroll=4)
+    lax.fori_loop(0, STEPS, advance, (volts0, flux0), unroll=8)
 
     reach = four_terms(dot(stack_hi_lo(cu[...]), x2[...], NT))
     placed = dot(stack_hi_lo(vo[...]), put, NT)
@@ -463,7 +496,7 @@
             dma((5,)),
             dma((HALVES,)),
             dma((2,)),
-            dma((rows,)),
+            dma((rows + 1,)),
             dma((zn + 2,)),
             dma((2,)),
             pltpu.SemaphoreType.REGULAR((max((subs - 1).bit_length() - 1, 1),)),

time: 27 us -> 26.6 us (0.985)
  Pallas kernels: 26.1 us -> 25.7 us
    pallas_call x1, Pallas kernels: 25.5 us -> 25.1 us  [on_device(): pl.pallas_call(functools.partial(kernel, subs, rows, ports, slice_len, ar...]
where the time goes in v6:
time: 26.6 us; the launch traced here: 26.4 us
  Pallas kernels  25.7 us (97%)
  between operations  0.64 us (2%)
    pallas_call x1, Pallas kernels, on_device(): pl.pallas_call(functools.partial(kernel, subs, rows, ports, slice_len, ar...  25.1 us
    pallas_call x1, Pallas kernels, on_device(): pl.pallas_call(give, out_shape=(jax.ShapeDtypeStruct((1, STEPS, ports), F...  0.6 us

profile of v6, /device:TPU:0, one launch (start us, length us, event | category | flops | bytes accessed | tf_op | source)
XLA Modules:
  0.0 26.4 jit_solution(718593269360589278)
XLA Ops:
  0.6 25.1 %window.1.both = f32[24,128]{1,0:T(8,128)S(1)} custom-call(f32[1,128,12288]{2,1,0:T(8,128)} %inv.1, f32[1,16,1536]{2,1,0:T(8,128)} %src.1, f32[1,32,128]{2,1,0:T(8,128)} %refs_0_.1, s32[1,128]{1,0:T(1,128)} %refs_1_.1, s32[1,128]{1,0:T(1,128)} %refs_2_.1, s32[1,128]{1,0:T(1,128)} %refs_3_.1, f32[1,128]{1,0:T(1,128)} %refs_4_.1, f32[1,128]{1,0:T(1,128)} %refs_5_.1, ...), custom_call_target="tpu_custom_call" | custom-call | tf_op jit(solution)/shard_map/window/pallas_call | solution.py:471
  25.8 0.6 %give.1 = (f32[1,16,128]{2,1,0:T(8,128)}, f32[1,128]{1,0:T(1,128)}) custom-call(f32[24,128]{1,0:T(8,128)S(1)} %window.1.both), custom_call_target="tpu_custom_call" | custom-call | tf_op jit(solution)/shard_map/give/pallas_call | solution.py:510

commit v7 on v6

--- a/solution.py
+++ b/solution.py
@@ -69,7 +69,6 @@
     total = rows * elems
     halves = total // LANES
     peers = subs - 1
-    turns = 2 * (zn - 1)
 
     barrier = pltpu.get_barrier_semaphore()
     for j in range(1, rows):
@@ -252,6 +251,10 @@
     def columns(b, count):
         return pl.ds(pl.multiple_of(b * slice_len, LANES), count * slice_len)
 
+    def chip_term(zb):
+        both = jnp.concatenate([gath[zb * 2], gath[zb * 2 + 1]], axis=1)
+        return dot(stack_hi_lo(both), m2[:, columns(zb * 2, 2)], NT)
+
     def use_sources(b):
         acc[...] += dot(stack_hi_lo(gath[b]), m2[:, columns(b, 1)], NT)
 
@@ -259,8 +262,7 @@
         inv_copy(h).wait()
         lax.fori_loop(h * rows // HALVES, (h + 1) * rows // HALVES, split_block, 0)
     pass_copy(partner).wait_recv()
-    home = jnp.concatenate([gath[z * 2], gath[z * 2 + 1]], axis=1)
-    acc[...] = dot(stack_hi_lo(home), m2[:, columns(z * 2, 2)], NT)
+    acc[...] = chip_term(z)
 
     for k in range(len(bits) - 1):
         pl.semaphore_wait(sub_in.at[k], len(bits))
@@ -274,18 +276,17 @@
         unit_copy(zz, zn, partner).start()
         send_subs(zz)
 
+    low_z = jnp.minimum(z, zn - 1 - z)
+    one = jnp.minimum(z + 1, 1)
+
     def other_chips(lo, hi, act):
         def body(q, carry):
-            i = jnp.where(jnp.logical_or(z == 0, z == zn - 1), turns - 1 - q, q)
-            zb = jnp.where(i % 2 == 0, z - i // 2 - 1, z + i // 2 + 1)
-
-            @pl.when(jnp.logical_and(jnp.logical_and(zb >= 0, zb < zn), zb != znear))
-            def _():
-                act(zb)
-
+            inside = jnp.where(q < low_z, low_z - 1 - q, q + 2)
+            zb = jnp.where(low_z == 0, zn - 1 - q, inside)
+            act(jnp.where(z < zn // 2, zb, zn - 1 - zb))
             return carry
 
-        lax.fori_loop(lo, hi, body, 0)
+        lax.fori_loop(lo, hi - 1 + one, body, 0)
 
     def take(zb):
         line_copy(zb * 2 + c, partner).wait_recv()
@@ -299,7 +300,7 @@
         use_sources(zb * 2 + 1 - c)
 
     near = znear * 2 + c
-    outer = jnp.where(lower, z - 1, z + 1) * 2 + c
+    outer = jnp.where(lower, z - 1, z + 1) * 2 + 1
 
     @pl.when(relays)
     def _():
@@ -338,9 +339,12 @@
 
     def take_use(zb):
         take(zb)
-        use_own(zb)
-
-    other_chips(0, 2, take_use)
+
+        @pl.when(c == 1)
+        def _():
+            use_own(zb)
+
+    other_chips(0, 1, take_use)
     arrived(got_units.at[c], sub_sem.at[1])
     both_copy(c).start()
 
@@ -361,11 +365,50 @@
         hacc[...] += dot(jnp.concatenate(split, axis=0), land, NT)
 
     use_records(c)
-    other_chips(2, turns, take_use)
-    other_chips(0, 2, use_passed)
+    at_end = jnp.logical_or(z == 0, z == zn - 1)
+
+    def relayed_chip(zb):
+        return jnp.logical_and(at_end, jnp.abs(z - zb) == 2)
+
+    def last_take(zb):
+        @pl.when(jnp.logical_and(relayed_chip(zb), c == 1))
+        def _():
+            for p in (1, 0):
+                line_copy(zb * 2 + p, partner).wait_recv()
+                pass_copy(zb * 2 + p).start()
+
+        @pl.when(jnp.logical_not(relayed_chip(zb)))
+        def _():
+            take(zb)
+
+    def first_chip(zb):
+        pass_copy(zb * 2 + 1).wait_recv()
+        acc[...] += chip_term(zb)
+
+    def last_chip(zb):
+        @pl.when(jnp.logical_and(relayed_chip(zb), c == 0))
+        def _():
+            pass_copy(zb * 2).wait_recv()
+
+        @pl.when(jnp.logical_not(jnp.logical_and(relayed_chip(zb), c == 1)))
+        def _():
+            pass_copy(zb * 2 + 1 - c).wait_recv()
+
+        acc[...] += chip_term(zb)
+
+    @pl.when(c == 0)
+    def _():
+        other_chips(0, 1, first_chip)
+
+    other_chips(1, zn - 2, last_take)
+
+    @pl.when(c == 1)
+    def _():
+        other_chips(0, 1, use_passed)
+
     both_copy(1 - c).wait_recv()
     use_records(1 - c)
-    other_chips(2, turns, use_passed)
+    other_chips(1, zn - 2, last_chip)
 
     landed = jnp.concatenate(
         [
@@ -404,7 +447,12 @@
 
     sent(got_units.at[c], sub_sem.at[0])
     sent(got_units.at[c], both_sem.at[0])
-    sent(gath.at[pl.ds(0, zn)], line_sem.at[1])
+    passes = zn + at_end.astype(jnp.int32) * (2 * c - 1)
+    for n in range(zn - 1, zn + 2):
+        @pl.when(passes == n)
+        def _():
+            sent(gath.at[pl.ds(0, n)], line_sem.at[1])
+
     line_sends = zn - 1 + relays.astype(jnp.int32) - skips.astype(jnp.int32)
     for n in range(zn - 2, zn + 1):
         @pl.when(line_sends == n)

time: 26.6 us -> 26.4 us (level)
  no operation moved by 1% of the time
where the time goes in v7:
time: 26.4 us; the launch traced here: 26.1 us
  Pallas kernels  25.5 us (97%)
  between operations  0.64 us (2%)
    pallas_call x1, Pallas kernels, on_device(): pl.pallas_call(functools.partial(kernel, subs, rows, ports, slice_len, ar...  24.9 us
    pallas_call x1, Pallas kernels, on_device(): pl.pallas_call(give, out_shape=(jax.ShapeDtypeStruct((1, STEPS, ports), F...  0.6 us

profile of v7, /device:TPU:0, one launch (start us, length us, event | category | flops | bytes accessed | tf_op | source)
XLA Modules:
  0.0 26.1 jit_solution(4478835661625252762)
XLA Ops:
  0.6 24.9 %window.1.both = f32[24,128]{1,0:T(8,128)S(1)} custom-call(f32[1,128,12288]{2,1,0:T(8,128)} %inv.1, f32[1,16,1536]{2,1,0:T(8,128)} %src.1, f32[1,32,128]{2,1,0:T(8,128)} %refs_0_.1, s32[1,128]{1,0:T(1,128)} %refs_1_.1, s32[1,128]{1,0:T(1,128)} %refs_2_.1, s32[1,128]{1,0:T(1,128)} %refs_3_.1, f32[1,128]{1,0:T(1,128)} %refs_4_.1, f32[1,128]{1,0:T(1,128)} %refs_5_.1, ...), custom_call_target="tpu_custom_call" | custom-call | tf_op jit(solution)/shard_map/window/pallas_call | solution.py:519
  25.5 0.6 %give.1 = (f32[1,16,128]{2,1,0:T(8,128)}, f32[1,128]{1,0:T(1,128)}) custom-call(f32[24,128]{1,0:T(8,128)S(1)} %window.1.both), custom_call_target="tpu_custom_call" | custom-call | tf_op jit(solution)/shard_map/give/pallas_call | solution.py:558
